TPU v7x, 256 devices: a whole 4x4x8 slice. The times are simulated.
256 devices in a mesh: row: 32 (over z, x), col: 8 (over y, core).
Axes of the slice: x: 4, y: 4, z: 8, core: 2. Of those that a mesh axis runs over, the one named last changes fastest.
Arguments:
- rhs: float32 [384, 512, 512], P('col', 'row'), may hold values from -6 to 6
- lower: float32 [384], replicated, may hold values from 0.5 to 2
- upper: float32 [384], replicated, may hold values from 0.5 to 2
Outputs:
- pressure: float32 [384, 512, 512], P('col', 'row')
All inputs are finite; a program needn't handle non-finite values.
Results may differ from a plain program's by a relative error of at most 0.0003.
Values sent between devices are 32-bit elements; how exact they have to be, the bound alone decides.
No kernel may reach another device: no remote copies, remote signals or barrier semaphores. Data moves between devices by JAX's collectives and lax.ppermute only.
A program may use at most 64 MiB of HBM per device.

v0:
```python
import math

import jax
import jax.numpy as jnp
import ml_dtypes
import numpy as np
from jax import lax
from jax.experimental import pallas as pl
from jax.experimental.pallas import tpu as pltpu
from jax.sharding import PartitionSpec as P

stream_weight = 0.04
span_weight = 0.16
shift_value = 0.0002


def split_table(values):
    high = values.astype(ml_dtypes.bfloat16)
    low = (values - high.astype(np.float64)).astype(ml_dtypes.bfloat16)
    return jnp.asarray(high), jnp.asarray(low)


def stream_table(nx_len, groups):
    modes = nx_len // 2 // groups
    points = np.arange(nx_len)
    wave = np.arange(groups * modes).reshape(groups, 1, modes, 1)
    angle = 2.0 * math.pi / nx_len * (wave * points % nx_len)
    table = np.concatenate([np.cos(angle), -np.sin(angle)], axis=1)
    return split_table(table.reshape(nx_len, nx_len))


def span_table(nz_len):
    half = nz_len // 2
    points = np.arange(nz_len)[:, None]
    wave = np.arange(half)[None, :]
    angle = 2.0 * math.pi / nz_len * (points * wave % nz_len)
    sines = np.sin(angle)
    sines[:, 0] = np.where(np.arange(nz_len) % 2 == 0, 1.0, -1.0)
    return split_table(np.concatenate([np.cos(angle), sines], axis=1))


def wave_square(stream_index, span_index, nx_len, nz_len):
    stream_angle = 2.0 * math.pi / nx_len * stream_index.astype(jnp.float32)
    span_angle = 2.0 * math.pi / nz_len * span_index.astype(jnp.float32)
    stream_part = stream_weight * (2.0 - 2.0 * jnp.cos(stream_angle))
    span_part = span_weight * (2.0 - 2.0 * jnp.cos(span_angle))
    return stream_part[:, None] + span_part[None, :]


def halves(values):
    high = values.astype(jnp.bfloat16)
    low = (values - high.astype(jnp.float32)).astype(jnp.bfloat16)
    return high, low


def dot3(a_high, a_low, b_high, b_low, dims):
    def one(a, b):
        return lax.dot_general(a, b, (dims, ((), ())), preferred_element_type=jnp.float32)

    return one(a_high, b_high) + (one(a_high, b_low) + one(a_low, b_high))


def swap_groups(tiles, width):
    count = len(tiles)
    lanes = count * width
    tiles = list(tiles)
    group = lax.broadcasted_iota(jnp.int32, tiles[0].shape, 1) // width
    bit = count // 2
    while bit:
        upper = (group & bit) != 0
        for first in range(count):
            if first & bit:
                continue
            a, b = tiles[first], tiles[first | bit]
            tiles[first] = jnp.where(upper, pltpu.roll(b, width * bit, 1), a)
            tiles[first | bit] = jnp.where(upper, b, pltpu.roll(a, lanes - width * bit, 1))
        bit //= 2
    return tiles


def both(values):
    return jnp.concatenate([values, values], axis=0)


def stream_forward(rhs_ref, high_ref, low_ref, out_ref):
    rows, span, nx_len = rhs_ref.shape
    high, low = halves(rhs_ref[...].reshape(rows * span, nx_len))
    out = dot3(high_ref[...], low_ref[...], high, low, ((1,), (1,)))
    out_ref[...] = out.reshape(out_ref.shape)


def stream_inverse(piece_ref, high_ref, low_ref, out_ref):
    groups, parts, cells = piece_ref.shape
    flat = piece_ref[...].reshape(groups * parts, cells)
    high, low = halves(flat.T)
    out = dot3(high, low, high_ref[...], low_ref[...], ((1,), (0,)))
    out_ref[...] = out.reshape(out_ref.shape)


def factor(place_ref, lower_ref, upper_ref, waves_ref, down_ref, up_ref, carry_down_ref, carry_up_ref, close_ref, start_ref):
    rows = down_ref.shape[0]
    blocks = carry_down_ref.shape[0]
    total = rows * blocks
    sigma = waves_ref[...]
    one = jnp.ones_like(sigma)
    step = 8

    def step_down(row, numer, denom):
        numer = lower_ref[row] * numer + sigma * denom
        return numer, numer + upper_ref[row] * denom

    def step_up(row, numer, denom):
        numer = upper_ref[row] * numer + sigma * denom
        return numer, numer + lower_ref[row] * denom

    def block(index, carry):
        t_down, t_up = carry
        other = blocks - 1 - index
        start_ref[0, index] = t_down
        start_ref[1, other] = t_up

        def some(chunk, inner):
            nd, dd, nu, du, prod_l, prod_u = inner
            for k in range(step):
                row = index * rows + chunk * step + k
                back = total - 1 - row
                nd, dd = step_down(row, nd, dd)
                nu, du = step_up(back, nu, du)
                prod_l = prod_l * lower_ref[row]
                prod_u = prod_u * upper_ref[back]
            return nd, dd, nu, du, prod_l, prod_u

        unit = jnp.float32(1.0)
        nd, dd, nu, du, prod_l, prod_u = lax.fori_loop(
            0, rows // step, some, (t_down, one, t_up, one, unit, unit)
        )
        inv_d = 1.0 / dd
        inv_u = 1.0 / du
        carry_down_ref[index] = prod_l * inv_d
        carry_up_ref[other] = prod_u * inv_u
        return nd * inv_d, nu * inv_u

    lax.fori_loop(0, blocks, block, (one, one))
    place = place_ref[1]
    first = place * rows

    def own(chunk, inner):
        nd, dd, nu, du = inner
        for k in range(step):
            row = chunk * step + k
            back = rows - 1 - row
            nd, new_d = step_down(first + row, nd, dd)
            down_ref[row] = dd / new_d
            nu, new_u = step_up(first + back, nu, du)
            up_ref[back] = du / new_u
            dd, du = new_d, new_u
        return nd, dd, nu, du

    nd, dd, nu, du = lax.fori_loop(
        0, rows // step, own, (start_ref[0, place], one, start_ref[1, place], one)
    )
    t_end = nd / dd
    t_next = start_ref[1, place]
    is_last = place == blocks - 1
    inner = jnp.where(is_last, 0.0, 1.0 / (t_next + t_end * (1.0 - t_next)))
    close_ref[0] = inner
    close_ref[1] = inner * (1.0 - t_next)


def span_forward(place_ref, lower_ref, upper_ref, piece_ref, high_ref, low_ref, down_ref, up_ref, rows_ref, send_ref, left_high, left_low, keep_ref):
    groups, parts, cells = piece_ref.shape
    some, _, nz_len = rows_ref.shape
    rows = keep_ref.shape[0]
    width = nz_len // groups
    count = 128 // width
    for octet in range(some // count):
        for tile in range(groups // count):
            tiles = [piece_ref[tile * count + s, :, octet * 128 : octet * 128 + 128] for s in range(count)]
            tiles = swap_groups(tiles, width)
            for j in range(count):
                high, low = halves(tiles[j])
                row = (octet * count + j) * parts
                left_high[row : row + parts, tile * 128 : tile * 128 + 128] = high
                left_low[row : row + parts, tile * 128 : tile * 128 + 128] = low
    spec = dot3(left_high[...], left_low[...], high_ref[...], low_ref[...], ((1,), (0,)))
    spec = spec.reshape(some, parts, nz_len)
    part = lax.broadcasted_iota(jnp.int32, (parts, nz_len), 0)
    wave = lax.broadcasted_iota(jnp.int32, (parts, nz_len), 1)
    single_x = (part % (parts // 2) == 0) & (place_ref[0] == 0)
    single_z = wave % (nz_len // 2) == 0
    base = 1.0 / (nz_len * nz_len)
    scale = jnp.where(single_x, base, 2.0 * base) * jnp.where(single_z, 1.0, 2.0)
    spec = spec * scale[None]
    rows_ref[...] = spec
    index = pl.program_id(0)
    keep_ref[pl.ds(index * some, some)] = spec

    @pl.when(index == pl.num_programs(0) - 1)
    def _():
        first = place_ref[1] * rows
        step = 8

        def sweep(chunk, carry):
            down, up = carry
            for k in range(step):
                row = chunk * step + k
                back = rows - 1 - row
                down = (lower_ref[first + row] * down - keep_ref[row]) * both(down_ref[row])
                up = (upper_ref[first + back] * up - keep_ref[back]) * both(up_ref[back])
            return down, up

        zero = jnp.zeros((parts, nz_len), jnp.float32)
        down, up = lax.fori_loop(0, rows // step, sweep, (zero, zero))
        for target in range(send_ref.shape[0]):
            send_ref[target] = jnp.where(target > place_ref[1], down, up)


def span_inverse(place_ref, lower_ref, upper_ref, rows_ref, down_ref, ends_ref, carry_down_ref, carry_up_ref, close_ref, high_ref, low_ref, out_ref, grow_ref, left_high, left_low):
    groups, parts, cells = out_ref.shape
    rows, _, nz_len = rows_ref.shape
    blocks = ends_ref.shape[0]
    width = nz_len // groups
    count = 128 // width
    index = pl.program_id(0)

    @pl.when(index == 0)
    def _():
        place = place_ref[1]
        first = place * rows
        step = 8
        zero = jnp.zeros((parts, nz_len), jnp.float32)
        before = lax.fori_loop(
            0, place, lambda k, value: ends_ref[k] + both(carry_down_ref[k]) * value, zero
        )

        def climb(k, value):
            other = blocks - 1 - k
            return ends_ref[other] + both(carry_up_ref[other]) * value

        after = lax.fori_loop(0, blocks - 1 - place, climb, zero)

        def descend(chunk, value):
            for k in range(step):
                row = chunk * step + k
                value = (lower_ref[first + row] * value - rows_ref[row]) * both(down_ref[row])
                grow_ref[row] = value
            return value

        last = lax.fori_loop(0, rows // step, descend, before)
        beyond = both(close_ref[0]) * after + both(close_ref[1]) * last

        def ascend(chunk, value):
            for k in range(step):
                row = rows - 1 - (chunk * step + k)
                ratio = upper_ref[first + row] * down_ref[row]
                value = grow_ref[row] + both(ratio) * value
                high, low = halves(value)
                place_row = pl.multiple_of(row * parts, parts)
                left_high[pl.ds(place_row, parts)] = high
                left_low[pl.ds(place_row, parts)] = low
            return value

        lax.fori_loop(0, rows // step, ascend, beyond)

    some = cells // width
    start = pl.multiple_of(index * some * parts, some * parts)
    back = dot3(
        left_high[pl.ds(start, some * parts)],
        left_low[pl.ds(start, some * parts)],
        high_ref[...],
        low_ref[...],
        ((1,), (1,)),
    )
    for octet in range(some // count):
        for tile in range(groups // count):
            tiles = []
            for j in range(count):
                row = (octet * count + j) * parts
                tiles.append(back[row : row + parts, tile * 128 : tile * 128 + 128])
            tiles = swap_groups(tiles, width)
            for s in range(count):
                out_ref[tile * count + s, :, octet * 128 : octet * 128 + 128] = tiles[s]


smem = pl.BlockSpec(memory_space=pltpu.SMEM)


def whole(shape):
    return pl.BlockSpec(shape, lambda *_: (0,) * len(shape))


def local(rhs, lower, upper):
    rows, span, nx_len = rhs.shape
    groups = lax.axis_size("row")
    blocks = lax.axis_size("col")
    nz_len = span * groups
    modes = nx_len // 2 // groups
    parts = 2 * modes
    steps = 3
    some = rows // steps
    cells = some * span
    place = jnp.stack([lax.axis_index("row"), lax.axis_index("col")]).astype(jnp.int32)
    stream_high, stream_low = stream_table(nx_len, groups)
    span_high, span_low = span_table(nz_len)
    table_x = whole((nx_len, nx_len))
    table_z = whole((nz_len, nz_len))
    f32 = jnp.float32
    piece_shape = jax.ShapeDtypeStruct((groups, parts, rows * span), f32)
    piece_spec = pl.BlockSpec((groups, parts, cells), lambda i: (0, 0, i))
    field_shape = jax.ShapeDtypeStruct((rows, span, nx_len), f32)
    field_spec = pl.BlockSpec((some, span, nx_len), lambda i: (i, 0, 0))
    mode_shape = jax.ShapeDtypeStruct((rows, parts, nz_len), f32)
    mode_spec = pl.BlockSpec((some, parts, nz_len), lambda i: (i, 0, 0))
    half_spec = whole((rows, modes, nz_len))
    carry_spec = whole((blocks, modes, nz_len))
    ends_shape = jax.ShapeDtypeStruct((blocks, parts, nz_len), f32)
    ends_spec = whole((blocks, parts, nz_len))

    send = pl.pallas_call(
        stream_forward,
        grid=(steps,),
        in_specs=[field_spec, table_x, table_x],
        out_specs=piece_spec,
        out_shape=piece_shape,
        name="stream_forward",
    )(rhs, stream_high, stream_low)
    piece = lax.all_to_all(send, "row", split_axis=0, concat_axis=0, tiled=True)

    stream_index = place[0] * modes + jnp.arange(modes)
    wave = jnp.arange(nz_len) % (nz_len // 2)
    span_index = jnp.where(jnp.arange(nz_len) == nz_len // 2, nz_len // 2, wave)
    sigma = wave_square(stream_index, span_index, nx_len, nz_len) + shift_value
    down, up, carry_down, carry_up, close = pl.pallas_call(
        factor,
        in_specs=[smem, smem, smem, whole((modes, nz_len))],
        out_specs=[half_spec, half_spec, carry_spec, carry_spec, whole((2, modes, nz_len))],
        out_shape=[
            jax.ShapeDtypeStruct((rows, modes, nz_len), f32),
            jax.ShapeDtypeStruct((rows, modes, nz_len), f32),
            jax.ShapeDtypeStruct((blocks, modes, nz_len), f32),
            jax.ShapeDtypeStruct((blocks, modes, nz_len), f32),
            jax.ShapeDtypeStruct((2, modes, nz_len), f32),
        ],
        grid=(1,),
        scratch_shapes=[pltpu.VMEM((2, blocks, modes, nz_len), f32)],
        name="factor",
    )(place, lower, upper, sigma)

    left = pltpu.VMEM((some * parts, nz_len), jnp.bfloat16)
    modes_rows, ends = pl.pallas_call(
        span_forward,
        grid=(steps,),
        in_specs=[smem, smem, smem, piece_spec, table_z, table_z, half_spec, half_spec],
        out_specs=[mode_spec, ends_spec],
        out_shape=[mode_shape, ends_shape],
        scratch_shapes=[left, left, pltpu.VMEM((rows, parts, nz_len), f32)],
        name="span_forward",
    )(place, lower, upper, piece, span_high, span_low, down, up)
    ends = lax.all_to_all(ends, "col", split_axis=0, concat_axis=0, tiled=True)

    left = pltpu.VMEM((rows * parts, nz_len), jnp.bfloat16)
    send = pl.pallas_call(
        span_inverse,
        grid=(steps,),
        in_specs=[smem, smem, smem, whole((rows, parts, nz_len)), half_spec, ends_spec, carry_spec, carry_spec, whole((2, modes, nz_len)), table_z, table_z],
        out_specs=piece_spec,
        out_shape=piece_shape,
        scratch_shapes=[pltpu.VMEM((rows, parts, nz_len), f32), left, left],
        name="span_inverse",
    )(place, lower, upper, modes_rows, down, ends, carry_down, carry_up, close, span_high, span_low)
    piece = lax.all_to_all(send, "row", split_axis=0, concat_axis=0, tiled=True)

    return pl.pallas_call(
        stream_inverse,
        grid=(steps,),
        in_specs=[piece_spec, table_x, table_x],
        out_specs=field_spec,
        out_shape=field_shape,
        name="stream_inverse",
    )(piece, stream_high, stream_low)


def solution(mesh):
    return jax.shard_map(
        local,
        mesh=mesh,
        in_specs=(P("col", "row", None), P(), P()),
        out_specs=P("col", "row", None),
        check_vma=False,
    )
```

profile of v0, /device:TPU:32, one launch (start us, length us, event | category | flops | bytes accessed | tf_op | source)
XLA Modules:
  0.0 131.1 jit_solution(7544398911569737676)
XLA Ops:
  0.0 4.6 %stream_forward.1 = f32[32,16,768]{2,1,0:T(8,128)} custom-call(f32[48,16,512]{2,1,0:T(8,128)} %rhs_ref.1, bf16[512,512]{1,0:T(8,128)(2,1)} %constant.48.clone.high_ref, bf16[512,512]{1,0:T(8,128)(2,1)} %constant.49.clone.low_ref), custom_call_target="tpu_custom_call" | custom-call | tf_op jit(solution)/shard_map/stream_forward/pallas_call | solution.py:319
  4.6 11.2 %all-to-all-start = ((f32[32,16,768]{2,1,0:T(8,128)}), f32[32,16,768]{2,1,0:T(8,128)S(1)}, u32[]{:S(2)}, u32[]{:S(2)}) async-start(f32[32,16,768]{2,1,0:T(8,128)} %stream_forward.1), calls=%async_computation | async-start | bytes 3145728 | tf_op jit(solution)/shard_map/all_to_all | solution.py:327
  15.9 0.6 pad_add_fusion.place_ref
  16.5 0.7 add_add_fusion.waves_ref
  17.2 5.1 %factor.1 = (f32[48,8,512]{2,1,0:T(8,128)}, f32[48,8,512]{2,1,0:T(8,128)}, f32[8,8,512]{2,1,0:T(8,128)}, f32[8,8,512]{2,1,0:T(8,128)}, f32[2,8,512]{2,1,0:T(8,128)}) custom-call(s32[2]{0:T(128)} %pad_add_fusion.place_ref, f32[384]{0:T(512)} %lower_ref.5, f32[384]{0:T(512)} %upper_ref.5, f32[8,512]{1,0:T(8,128)} %add_add_fusion.waves_ref), custom_call_target="tpu_custom_call" | custom-call | tf_op jit(solution)/shard_map/factor/pallas_call | solution.py:333
  22.3 32.0 %all-to-all-done.piece_ref = f32[32,16,768]{2,1,0:T(8,128)S(1)} async-done(((f32[32,16,768]{2,1,0:T(8,128)}), f32[32,16,768]{2,1,0:T(8,128)S(1)}, u32[]{:S(2)}, u32[]{:S(2)}) %all-to-all-start) | async-done | bytes 1572896 | tf_op jit(solution)/shard_map/all_to_all | solution.py:327
  54.2 0.0 copy-start
  54.2 1.1 copy-done
  55.4 6.4 %span_forward.1 = (f32[48,16,512]{2,1,0:T(8,128)}, f32[8,16,512]{2,1,0:T(8,128)}) custom-call(s32[2]{0:T(128)} %pad_add_fusion.place_ref, f32[384]{0:T(512)} %lower_ref.5, f32[384]{0:T(512)} %upper_ref.5, f32[32,16,768]{2,1,0:T(8,128)} %copy-done, bf16[512,512]{1,0:T(8,128)(2,1)} %constant.50.clone.high_ref, bf16[512,512]{1,0:T(8,128)(2,1)} %constant.51.clone.low_ref, ...), custom_call_target="tpu_custom_call" | custom-call | tf_op jit(solution)/shard_map/span_forward/pallas_call | solution.py:350
  61.8 12.1 %all_to_all.15.ends_ref = f32[8,16,512]{2,1,0:T(8,128)} all-to-all(f32[8,16,512]{2,1,0:T(8,128)} %get-tuple-element.15), channel_id=1, replica_groups=mesh['row'=32,'col'=8] {'col'}, dimensions={0} | all-to-all | bytes 524288 | tf_op jit(solution)/shard_map/all_to_all | solution.py:359
  73.8 6.7 %span_inverse.1 = f32[32,16,768]{2,1,0:T(8,128)} custom-call(s32[2]{0:T(128)} %pad_add_fusion.place_ref, f32[384]{0:T(512)} %lower_ref.5, f32[384]{0:T(512)} %upper_ref.5, f32[48,16,512]{2,1,0:T(8,128)} %get-tuple-element.14.rows_ref, f32[48,8,512]{2,1,0:T(8,128)} %get-tuple-element.12.down_ref, f32[8,16,512]{2,1,0:T(8,128)} %all_to_all.15.ends_ref, ...), custom_call_target="tpu_custom_call" | custom-call | tf_op jit(solution)/shard_map/span_inverse/pallas_call | solution.py:362
  80.5 46.0 %all_to_all.16.piece_ref = f32[32,16,768]{2,1,0:T(8,128)} all-to-all(f32[32,16,768]{2,1,0:T(8,128)} %span_inverse.1), channel_id=1, replica_groups=mesh['row'=32,'col'=8] {'row'}, dimensions={0} | all-to-all | bytes 3145728 | tf_op jit(solution)/shard_map/all_to_all | solution.py:371
  126.5 4.6 %stream_inverse.1 = f32[48,16,512]{2,1,0:T(8,128)} custom-call(f32[32,16,768]{2,1,0:T(8,128)} %all_to_all.16.piece_ref, bf16[512,512]{1,0:T(8,128)(2,1)} %constant.48.clone.high_ref, bf16[512,512]{1,0:T(8,128)(2,1)} %constant.49.clone.low_ref), custom_call_target="tpu_custom_call" | custom-call | tf_op jit(solution)/shard_map/stream_inverse/pallas_call | solution.py:373
  (2 shorter events, 0.1 us)
Async XLA Ops:
  4.6 49.6 %all-to-all-start = ((f32[32,16,768]{2,1,0:T(8,128)}), f32[32,16,768]{2,1,0:T(8,128)S(1)}, u32[]{:S(2)}, u32[]{:S(2)}) async-start(f32[32,16,768]{2,1,0:T(8,128)} %stream_forward.1), calls=%async_computation | async-start | bytes 3145728 | tf_op jit(solution)/shard_map/all_to_all | solution.py:327
  54.2 1.1 copy-start
where the time goes:
time: 132 us; the launch traced here: 131 us
  blocking collectives  58 us (44%)
  waiting for transfers between devices  32 us (24%)
  Pallas kernels  27.4 us (21%)
  starting transfers between devices  11.2 us (8%)
  other arithmetic  1.36 us (1%)
    all_to_all x1, blocking collectives, local(): piece = lax.all_to_all(send, 'row', split_axis=0, concat_axis=0, tiled=True)  46 us
    all_to_all x1, waiting for transfers between devices, local(): piece = lax.all_to_all(send, 'row', split_axis=0, concat_axis=0, tiled=True)  32 us
    all_to_all x1, blocking collectives, local(): ends = lax.all_to_all(ends, 'col', split_axis=0, concat_axis=0, tiled=True)  12.1 us
    all_to_all x1, starting transfers between devices, local(): piece = lax.all_to_all(send, 'row', split_axis=0, concat_axis=0, tiled=True)  11.2 us
    pallas_call x1, Pallas kernels, local(): pl.pallas_call(span_inverse, grid=(steps,), in_specs=[smem, smem, smem, w...  6.67 us
    pallas_call x1, Pallas kernels, local(): pl.pallas_call(span_forward, grid=(steps,), in_specs=[smem, smem, smem, p...  6.39 us
    pallas_call x1, Pallas kernels, local(): pl.pallas_call(factor, in_specs=[smem, smem, smem, whole((modes, nz_len))...  5.07 us
    pallas_call x1, Pallas kernels, local(): pl.pallas_call(stream_inverse, grid=(steps,), in_specs=[piece_spec, table...  4.64 us
  transfers between devices with their start and end apart: 1, of which 1 were waited for; matrix products, arithmetic and copies ran while one was open for 1% of the time, Pallas kernels for 4%

commit v1 on v0

v1 whole, which is shorter than its diff:
```python
import math

import jax
import jax.numpy as jnp
import ml_dtypes
import numpy as np
from jax import lax
from jax.experimental import pallas as pl
from jax.experimental.pallas import tpu as pltpu
from jax.sharding import PartitionSpec as P

stream_weight = 0.04
span_weight = 0.16
shift_value = 0.0002


def split_table(values):
    high = values.astype(ml_dtypes.bfloat16)
    low = (values - high.astype(np.float64)).astype(ml_dtypes.bfloat16)
    return jnp.asarray(high), jnp.asarray(low)


def stream_table(nx_len, groups):
    half = nx_len // 2
    modes = half // groups
    points = np.arange(half)
    wave = 2 * np.arange(half // 2).reshape(1, -1, 1, modes, 1) + np.arange(2).reshape(2, 1, 1, 1, 1)
    angle = 2.0 * math.pi / nx_len * (wave * points % nx_len)
    table = np.concatenate([np.cos(angle), -np.sin(angle)], axis=2)
    return split_table(table.reshape(2, half, half))


def span_waves(nz_len):
    even = np.arange(0, nz_len // 2, 2)
    top = np.where(even == 0, nz_len // 2, even)
    return np.concatenate([even, top, even + 1, even + 1])


def span_table(nz_len):
    half = nz_len // 2
    points = np.arange(half)[:, None]
    wave = span_waves(nz_len)[None, :]
    angle = 2.0 * math.pi / nz_len * (points * wave % nz_len)
    index = np.arange(nz_len)[None, :]
    cosine = (index % half < half // 2) | (index == half // 2)
    table = np.where(cosine, np.cos(angle), np.sin(angle))
    return split_table(np.stack([table[:, :half], table[:, half:]]))


def wave_square(stream_index, span_index, nx_len, nz_len):
    stream_angle = 2.0 * math.pi / nx_len * stream_index.astype(jnp.float32)
    span_angle = 2.0 * math.pi / nz_len * span_index.astype(jnp.float32)
    stream_part = stream_weight * (2.0 - 2.0 * jnp.cos(stream_angle))
    span_part = span_weight * (2.0 - 2.0 * jnp.cos(span_angle))
    return stream_part[:, None] + span_part[None, :]


def halves(values):
    high = values.astype(jnp.bfloat16)
    low = (values - high.astype(jnp.float32)).astype(jnp.bfloat16)
    return high, low


def dot3(a_high, a_low, b_high, b_low, dims):
    def one(a, b):
        return lax.dot_general(a, b, (dims, ((), ())), preferred_element_type=jnp.float32)

    return one(a_high, b_high) + (one(a_high, b_low) + one(a_low, b_high))


def swap_groups(tiles, width):
    count = len(tiles)
    lanes = count * width
    tiles = list(tiles)
    group = lax.broadcasted_iota(jnp.int32, tiles[0].shape, 1) // width
    bit = count // 2
    while bit:
        upper = (group & bit) != 0
        for first in range(count):
            if first & bit:
                continue
            a, b = tiles[first], tiles[first | bit]
            tiles[first] = jnp.where(upper, pltpu.roll(b, width * bit, 1), a)
            tiles[first | bit] = jnp.where(upper, b, pltpu.roll(a, lanes - width * bit, 1))
        bit //= 2
    return tiles


def both(values):
    return jnp.concatenate([values, values], axis=0)


def stream_forward(rhs_ref, high_ref, low_ref, out_ref):
    rows, span, nx_len = rhs_ref.shape
    groups = out_ref.shape[0]
    cells = rows * span
    half = nx_len // 2
    field = rhs_ref[...].reshape(cells, nx_len)
    first, second = field[:, :half], field[:, half:]
    for parity, folded in enumerate((first + second, first - second)):
        high, low = halves(folded)
        out = dot3(high_ref[parity], low_ref[parity], high, low, ((1,), (1,)))
        place = parity * groups // 2
        out_ref[place : place + groups // 2] = out.reshape(groups // 2, -1, cells)


def stream_inverse(piece_ref, high_ref, low_ref, out_ref):
    rows, span, nx_len = out_ref.shape
    groups = piece_ref.shape[0]
    cells = rows * span
    half = nx_len // 2
    start = pl.multiple_of(pl.program_id(0) * cells, cells)
    outs = []
    for parity in range(2):
        place = parity * groups // 2
        flat = piece_ref[place : place + groups // 2, :, pl.ds(start, cells)].reshape(half, cells)
        high, low = halves(flat.T)
        outs.append(dot3(high, low, high_ref[parity], low_ref[parity], ((1,), (0,))))
    even, odd = outs
    out_ref[:, :, :half] = (even + odd).reshape(rows, span, half)
    out_ref[:, :, half:] = (even - odd).reshape(rows, span, half)


def factor(place_ref, lower_ref, upper_ref, waves_ref, both_ref, carry_down_ref, carry_up_ref, close_ref, start_ref):
    rows = both_ref.shape[1]
    blocks = carry_down_ref.shape[0]
    total = rows * blocks
    sigma = waves_ref[...]
    one = jnp.ones_like(sigma)
    step = 8

    def step_down(row, numer, denom):
        numer = lower_ref[row] * numer + sigma * denom
        return numer, numer + upper_ref[row] * denom

    def step_up(row, numer, denom):
        numer = upper_ref[row] * numer + sigma * denom
        return numer, numer + lower_ref[row] * denom

    def block(index, carry):
        t_down, t_up = carry
        other = blocks - 1 - index
        start_ref[0, index] = t_down
        start_ref[1, other] = t_up

        def some(chunk, inner):
            nd, dd, nu, du, prod_l, prod_u = inner
            for k in range(step):
                row = index * rows + chunk * step + k
                back = total - 1 - row
                nd, dd = step_down(row, nd, dd)
                nu, du = step_up(back, nu, du)
                prod_l = prod_l * lower_ref[row]
                prod_u = prod_u * upper_ref[back]
            return nd, dd, nu, du, prod_l, prod_u

        unit = jnp.float32(1.0)
        nd, dd, nu, du, prod_l, prod_u = lax.fori_loop(
            0, rows // step, some, (t_down, one, t_up, one, unit, unit)
        )
        inv_d = 1.0 / dd
        inv_u = 1.0 / du
        carry_down_ref[index] = prod_l * inv_d
        carry_up_ref[other] = prod_u * inv_u
        return nd * inv_d, nu * inv_u

    lax.fori_loop(0, blocks, block, (one, one))
    place = place_ref[1]
    first = place * rows

    def own(chunk, inner):
        nd, dd, nu, du = inner
        for k in range(step):
            row = chunk * step + k
            back = rows - 1 - row
            nd, new_d = step_down(first + row, nd, dd)
            both_ref[0, row] = dd / new_d
            nu, new_u = step_up(first + back, nu, du)
            both_ref[1, back] = du / new_u
            dd, du = new_d, new_u
        return nd, dd, nu, du

    nd, dd, nu, du = lax.fori_loop(
        0, rows // step, own, (start_ref[0, place], one, start_ref[1, place], one)
    )
    t_end = nd / dd
    t_next = start_ref[1, place]
    is_last = place == blocks - 1
    inner = jnp.where(is_last, 0.0, 1.0 / (t_next + t_end * (1.0 - t_next)))
    close_ref[0] = inner
    close_ref[1] = inner * (1.0 - t_next)


def span_forward(place_ref, lower_ref, upper_ref, piece_ref, high_ref, low_ref, factor_ref, rows_ref, send_ref, left_ref):
    groups, parts, cells = piece_ref.shape
    rows, _, nz_len = rows_ref.shape
    half = nz_len // 2
    width = nz_len // groups
    count = 128 // width
    some = left_ref.shape[1] // parts
    part = lax.broadcasted_iota(jnp.int32, (parts, half), 0)
    wave = lax.broadcasted_iota(jnp.int32, (parts, half), 1)
    single_x = (part % (parts // 2) == 0) & (place_ref[0] == 0)
    single_z = wave % (half // 2) == 0
    base = 1.0 / (nz_len * nz_len)
    scale_odd = jnp.where(single_x, 2.0 * base, 4.0 * base)
    scale_even = scale_odd * jnp.where(single_z, 0.5, 1.0)

    def transform(index, carry):
        for octet in range(some // count):
            lane = pl.multiple_of(index * (some * width) + octet * 128, 128)
            for tile in range(groups // count // 2):
                first = [piece_ref[tile * count + s, :, pl.ds(lane, 128)] for s in range(count)]
                second = [piece_ref[groups // 2 + tile * count + s, :, pl.ds(lane, 128)] for s in range(count)]
                for parity in range(2):
                    tiles = [a - b if parity else a + b for a, b in zip(first, second)]
                    tiles = swap_groups(tiles, width)
                    for j in range(count):
                        row = (octet * count + j) * parts
                        left_ref[parity, row : row + parts, tile * 128 : tile * 128 + 128] = tiles[j]
        for parity, scale in enumerate((scale_even, scale_odd)):
            high, low = halves(left_ref[parity])
            spec = dot3(high, low, high_ref[parity], low_ref[parity], ((1,), (0,)))
            spec = spec.reshape(some, parts, half) * scale[None]
            rows_ref[pl.ds(index * some, some), :, parity * half : parity * half + half] = spec
        return carry

    lax.fori_loop(0, rows // some, transform, 0)
    first = place_ref[1] * rows
    step = 8

    def sweep(chunk, carry):
        down, up = carry
        for k in range(step):
            row = chunk * step + k
            back = rows - 1 - row
            down = (lower_ref[first + row] * down - rows_ref[row]) * both(factor_ref[0, row])
            up = (upper_ref[first + back] * up - rows_ref[back]) * both(factor_ref[1, back])
        return down, up

    zero = jnp.zeros((parts, nz_len), jnp.float32)
    down, up = lax.fori_loop(0, rows // step, sweep, (zero, zero))
    for target in range(send_ref.shape[0]):
        send_ref[target] = jnp.where(target > place_ref[1], down, up)


def span_inverse(place_ref, lower_ref, upper_ref, rows_ref, factor_ref, ends_ref, carry_down_ref, carry_up_ref, close_ref, high_ref, low_ref, out_ref, grow_ref):
    groups, parts, cells = out_ref.shape
    rows, _, nz_len = rows_ref.shape
    blocks = ends_ref.shape[0]
    half = nz_len // 2
    width = nz_len // groups
    count = 128 // width
    some = 16
    place = place_ref[1]
    first = place * rows
    step = 8
    zero = jnp.zeros((parts, nz_len), jnp.float32)
    before = lax.fori_loop(
        0, place, lambda k, value: ends_ref[k] + both(carry_down_ref[k]) * value, zero
    )

    def climb(k, value):
        other = blocks - 1 - k
        return ends_ref[other] + both(carry_up_ref[other]) * value

    after = lax.fori_loop(0, blocks - 1 - place, climb, zero)

    def descend(chunk, value):
        for k in range(step):
            row = chunk * step + k
            value = (lower_ref[first + row] * value - rows_ref[row]) * both(factor_ref[0, row])
            grow_ref[row] = value
        return value

    last = lax.fori_loop(0, rows // step, descend, before)
    beyond = both(close_ref[0]) * after + both(close_ref[1]) * last

    def ascend(chunk, value):
        for k in range(step):
            row = rows - 1 - (chunk * step + k)
            ratio = upper_ref[first + row] * factor_ref[0, row]
            value = grow_ref[row] + both(ratio) * value
            grow_ref[row] = value
        return value

    lax.fori_loop(0, rows // step, ascend, beyond)

    def transform(index, carry):
        backs = []
        for parity in range(2):
            left = grow_ref[pl.ds(index * some, some), :, parity * half : parity * half + half]
            high, low = halves(left.reshape(some * parts, half))
            backs.append(dot3(high, low, high_ref[parity], low_ref[parity], ((1,), (1,))))
        even, odd = backs
        for part, back in enumerate((even + odd, even - odd)):
            for octet in range(some // count):
                lane = pl.multiple_of(index * (some * width) + octet * 128, 128)
                for tile in range(groups // count // 2):
                    tiles = []
                    for j in range(count):
                        row = (octet * count + j) * parts
                        tiles.append(back[row : row + parts, tile * 128 : tile * 128 + 128])
                    tiles = swap_groups(tiles, width)
                    for s in range(count):
                        out_ref[part * groups // 2 + tile * count + s, :, pl.ds(lane, 128)] = tiles[s]
        return carry

    lax.fori_loop(0, rows // some, transform, 0)


smem = pl.BlockSpec(memory_space=pltpu.SMEM)


vmem = pl.BlockSpec(memory_space=pltpu.VMEM)


def local(rhs, lower, upper):
    rows, span, nx_len = rhs.shape
    groups = lax.axis_size("row")
    blocks = lax.axis_size("col")
    nz_len = span * groups
    modes = nx_len // 2 // groups
    parts = 2 * modes
    steps = 3
    some = rows // steps
    place = jnp.stack([lax.axis_index("row"), lax.axis_index("col")]).astype(jnp.int32)
    stream_high, stream_low = stream_table(nx_len, groups)
    span_high, span_low = span_table(nz_len)
    f32 = jnp.float32
    params = pltpu.CompilerParams(vmem_limit_bytes=16 * 1024 * 1024)

    def on_chip(*shape):
        return pltpu.VMEM(shape, f32)

    def on_hbm(value):
        return pltpu.with_memory_space_constraint(value, pltpu.HBM)

    table_spec = pl.BlockSpec((2, nx_len // 2, nx_len // 2), lambda i: (0, 0, 0))
    field_spec = pl.BlockSpec((some, span, nx_len), lambda i: (i, 0, 0))
    piece_shape = on_chip(groups, parts, rows * span)

    def exchange(value, axis):
        return lax.all_to_all(value, axis, split_axis=0, concat_axis=0, tiled=True)

    send = pl.pallas_call(
        stream_forward,
        grid=(steps,),
        in_specs=[field_spec, table_spec, table_spec],
        out_specs=pl.BlockSpec((groups, parts, some * span), lambda i: (0, 0, i)),
        out_shape=jax.ShapeDtypeStruct((groups, parts, rows * span), f32),
        compiler_params=params,
        name="stream_forward",
    )(on_hbm(rhs), on_hbm(stream_high), on_hbm(stream_low))
    piece = exchange(send, "row")

    order = place[0] * modes + jnp.arange(modes)
    quarter = nx_len // 4
    stream_index = 2 * (order % quarter) + order // quarter
    span_index = jnp.asarray(span_waves(nz_len).astype(np.int32))
    sigma = wave_square(stream_index, span_index, nx_len, nz_len) + shift_value
    factors, carry_down, carry_up, close = pl.pallas_call(
        factor,
        in_specs=[smem, smem, smem, vmem],
        out_specs=[vmem] * 4,
        out_shape=[
            on_chip(2, rows, modes, nz_len),
            on_chip(blocks, modes, nz_len),
            on_chip(blocks, modes, nz_len),
            on_chip(2, modes, nz_len),
        ],
        scratch_shapes=[on_chip(2, blocks, modes, nz_len)],
        compiler_params=params,
        name="factor",
    )(place, lower, upper, sigma)

    mode_rows, ends = pl.pallas_call(
        span_forward,
        in_specs=[smem, smem, smem] + [vmem] * 4,
        out_specs=[vmem, vmem],
        out_shape=[on_chip(rows, parts, nz_len), on_chip(blocks, parts, nz_len)],
        scratch_shapes=[on_chip(2, some * parts, nz_len // 2)],
        compiler_params=params,
        name="span_forward",
    )(place, lower, upper, piece, span_high, span_low, factors)
    ends = exchange(ends, "col")

    send = pl.pallas_call(
        span_inverse,
        in_specs=[smem, smem, smem] + [vmem] * 8,
        out_specs=vmem,
        out_shape=piece_shape,
        scratch_shapes=[on_chip(rows, parts, nz_len)],
        compiler_params=params,
        name="span_inverse",
    )(place, lower, upper, mode_rows, factors, ends, carry_down, carry_up, close, span_high, span_low)
    piece = exchange(send, "row")

    return pl.pallas_call(
        stream_inverse,
        grid=(steps,),
        in_specs=[vmem, vmem, vmem],
        out_specs=field_spec,
        out_shape=jax.ShapeDtypeStruct((rows, span, nx_len), f32),
        compiler_params=params,
        name="stream_inverse",
    )(piece, stream_high, stream_low)


def solution(mesh):
    return jax.shard_map(
        local,
        mesh=mesh,
        in_specs=(P("col", "row", None), P(), P()),
        out_specs=P("col", "row", None),
        check_vma=False,
    )
```

time: 132 us -> 122 us (0.924)
  Pallas kernels: 27.4 us -> 17.3 us
    pallas_call x4, Pallas kernels: 22.8 us -> 13.2 us  [the longest x1 3.77 us: local(): pl.pallas_call(factor, in_specs=[smem, smem, smem, vmem], out_specs=[vmem...]
  transfers between devices with their start and end apart: 1 -> 1, of which waited for: 1 -> 1; matrix products, arithmetic and copies ran while one was open for 1% -> 0% of each run, Pallas kernels for 4% -> 3%
where the time goes in v1:
time: 122 us
  blocking collectives  57.6 us (47%)
  waiting for transfers between devices  33.1 us (27%)
  Pallas kernels  17.3 us (14%)
  starting transfers between devices  11.3 us (9%)
  local copies, waits for them, and re-layouts  2.24 us (2%)
    all_to_all x2, blocking collectives, exchange(): return lax.all_to_all(value, axis, split_axis=0, concat_axis=0, tiled=True)  57.6 us
    all_to_all x1, waiting for transfers between devices, exchange(): return lax.all_to_all(value, axis, split_axis=0, concat_axis=0, tiled=True)  33.1 us
    all_to_all x1, starting transfers between devices, exchange(): return lax.all_to_all(value, axis, split_axis=0, concat_axis=0, tiled=True)  11.3 us
    pallas_call x1, Pallas kernels, local(): pl.pallas_call(stream_forward, grid=(steps,), in_specs=[field_spec, table...  4.07 us
    pallas_call x1, Pallas kernels, local(): pl.pallas_call(factor, in_specs=[smem, smem, smem, vmem], out_specs=[vmem...  3.77 us
    pallas_call x1, Pallas kernels, local(): pl.pallas_call(span_inverse, in_specs=[smem, smem, smem] + [vmem] * 8, ou...  3.63 us
    pallas_call x1, Pallas kernels, local(): pl.pallas_call(span_forward, in_specs=[smem, smem, smem] + [vmem] * 4, ou...  3.22 us
    pallas_call x1, Pallas kernels, local(): pl.pallas_call(stream_inverse, grid=(steps,), in_specs=[vmem, vmem, vmem]...  2.59 us
  transfers between devices with their start and end apart: 1, of which 1 were waited for; matrix products, arithmetic and copies ran while one was open for 0% of the time, Pallas kernels for 3%

profile of v1, /device:TPU:32, one launch (start us, length us, event | category | flops | bytes accessed | tf_op | source)
XLA Modules:
  0.0 121.9 jit_solution(13688787640772134542)
XLA Ops:
  0.0 4.1 %stream_forward.1 = f32[32,16,768]{2,1,0:T(8,128)} custom-call(f32[48,16,512]{2,1,0:T(8,128)} %rhs_ref.1, bf16[2,256,256]{2,1,0:T(8,128)(2,1)} %constant.63.clone.high_ref, bf16[2,256,256]{2,1,0:T(8,128)(2,1)} %constant.64.clone.low_ref), custom_call_target="tpu_custom_call" | custom-call | tf_op jit(solution)/shard_map/stream_forward/pallas_call | solution.py:346
  4.1 0.0 copy-start.11
  4.1 0.0 copy-start.9
  4.1 0.0 copy-start.10
  4.1 0.0 copy-start.2
  4.1 11.3 %all-to-all-start = ((f32[32,16,768]{2,1,0:T(8,128)}), f32[32,16,768]{2,1,0:T(8,128)S(1)}, u32[]{:S(2)}, u32[]{:S(2)}) async-start(f32[32,16,768]{2,1,0:T(8,128)} %stream_forward.1), calls=%async_computation | async-start | bytes 3145728 | tf_op jit(solution)/shard_map/all_to_all | solution.py:344
  15.4 0.1 subtract_multiply_fusion
  15.5 0.1 pad_add_fusion.place_ref
  15.6 0.0 copy-done.11
  15.6 0.1 add_add_fusion.waves_ref
  15.6 0.0 copy-done.9
  15.6 0.0 copy-done.10
  15.7 3.8 %factor.1 = (f32[2,48,8,512]{3,2,1,0:T(8,128)S(1)}, f32[8,8,512]{2,1,0:T(8,128)S(1)}, f32[8,8,512]{2,1,0:T(8,128)S(1)}, f32[2,8,512]{2,1,0:T(8,128)S(1)}) custom-call(s32[2]{0:T(128)S(1)} %pad_add_fusion.place_ref, f32[384]{0:T(512)S(1)} %copy-done.9, f32[384]{0:T(512)S(1)} %copy-done.10, f32[8,512]{1,0:T(8,128)S(1)} %add_add_fusion.waves_ref), custom_call_target="tpu_custom_call" | custom-call | tf_op jit(solution)/shard_map/factor/pallas_call | solution.py:362
  19.4 0.0 copy-start.5
  19.4 0.6 copy-done.5
  20.1 0.0 copy-start.7
  20.1 0.6 copy-done.7
  20.7 33.1 %all-to-all-done.piece_ref = f32[32,16,768]{2,1,0:T(8,128)S(1)} async-done(((f32[32,16,768]{2,1,0:T(8,128)}), f32[32,16,768]{2,1,0:T(8,128)S(1)}, u32[]{:S(2)}, u32[]{:S(2)}) %all-to-all-start) | async-done | bytes 1572896 | tf_op jit(solution)/shard_map/all_to_all | solution.py:344
  53.8 0.0 copy-done.2
  53.8 0.0 copy-start.3
  53.8 0.9 copy-done.3
  54.8 0.0 copy-start.4
  54.8 0.0 copy-start.6
  54.8 0.0 copy-start.8
  54.8 3.2 %span_forward.1 = (f32[48,16,512]{2,1,0:T(8,128)S(1)}, f32[8,16,512]{2,1,0:T(8,128)S(1)}) custom-call(s32[2]{0:T(128)S(1)} %pad_add_fusion.place_ref, f32[384]{0:T(512)S(1)} %copy-done.9, f32[384]{0:T(512)S(1)} %copy-done.10, f32[32,16,768]{2,1,0:T(8,128)S(1)} %all-to-all-done.piece_ref, bf16[2,256,256]{2,1,0:T(8,128)(2,1)S(1)} %copy-done.3, ...), custom_call_target="tpu_custom_call" | custom-call | tf_op jit(solution)/shard_map/span_forward/pallas_call | solution.py:377
  58.0 11.8 %all_to_all.15.ends_ref = f32[8,16,512]{2,1,0:T(8,128)S(1)} all-to-all(f32[8,16,512]{2,1,0:T(8,128)S(1)} %get-tuple-element.13), channel_id=1, replica_groups=mesh['row'=32,'col'=8] {'col'}, dimensions={0} | all-to-all | bytes 524288 | tf_op jit(solution)/shard_map/all_to_all | solution.py:344
  69.8 0.0 copy-done.4
  69.8 0.0 copy-done.6
  69.8 0.0 copy-done.8
  69.8 3.6 %span_inverse.1 = f32[32,16,768]{2,1,0:T(8,128)S(1)} custom-call(s32[2]{0:T(128)S(1)} %pad_add_fusion.place_ref, f32[384]{0:T(512)S(1)} %copy-done.9, f32[384]{0:T(512)S(1)} %copy-done.10, f32[48,16,512]{2,1,0:T(8,128)S(1)} %get-tuple-element.12.rows_ref, f32[2,48,8,512]{3,2,1,0:T(8,128)S(1)} %get-tuple-element.11.factor_ref, ...), custom_call_target="tpu_custom_call" | custom-call | tf_op jit(solution)/shard_map/span_inverse/pallas_call | solution.py:388
  73.5 0.0 copy-start
  73.5 0.0 copy-start.1
  73.5 45.8 %all_to_all.16.piece_ref = f32[32,16,768]{2,1,0:T(8,128)S(1)} all-to-all(f32[32,16,768]{2,1,0:T(8,128)S(1)} %span_inverse.1), channel_id=1, replica_groups=mesh['row'=32,'col'=8] {'row'}, dimensions={0} | all-to-all | bytes 3145728 | tf_op jit(solution)/shard_map/all_to_all | solution.py:344
  119.3 0.0 copy-done
  119.3 0.0 copy-done.1
  119.3 2.6 %stream_inverse.1 = f32[48,16,512]{2,1,0:T(8,128)} custom-call(f32[32,16,768]{2,1,0:T(8,128)S(1)} %all_to_all.16.piece_ref, bf16[2,256,256]{2,1,0:T(8,128)(2,1)S(1)} %copy-done.1, bf16[2,256,256]{2,1,0:T(8,128)(2,1)S(1)} %copy-done), custom_call_target="tpu_custom_call" | custom-call | tf_op jit(solution)/shard_map/stream_inverse/pallas_call | solution.py:399
Async XLA Ops:
  4.1 11.5 %copy-start.11 = (f32[512]{0:T(512)S(1)}, f32[512]{0:T(512)}, u32[]{:S(2)}) copy-start(f32[512]{0:T(512)} %constant.74) | copy-start | bytes 6148
  4.1 11.6 %copy-start.9 = (f32[384]{0:T(512)S(1)}, f32[384]{0:T(512)}, u32[]{:S(2)}) copy-start(f32[384]{0:T(512)} %lower_ref.5) | copy-start | bytes 4612
  4.1 11.6 %copy-start.10 = (f32[384]{0:T(512)S(1)}, f32[384]{0:T(512)}, u32[]{:S(2)}) copy-start(f32[384]{0:T(512)} %upper_ref.5) | copy-start | bytes 4612
  4.1 49.8 %copy-start.2 = (bf16[2,256,256]{2,1,0:T(8,128)(2,1)S(1)}, bf16[2,256,256]{2,1,0:T(8,128)(2,1)}, u32[]{:S(2)}) copy-start(bf16[2,256,256]{2,1,0:T(8,128)(2,1)} %constant.66.clone.low_ref) | copy-start | bytes 786436
  4.1 49.7 %all-to-all-start = ((f32[32,16,768]{2,1,0:T(8,128)}), f32[32,16,768]{2,1,0:T(8,128)S(1)}, u32[]{:S(2)}, u32[]{:S(2)}) async-start(f32[32,16,768]{2,1,0:T(8,128)} %stream_forward.1), calls=%async_computation | async-start | bytes 3145728 | tf_op jit(solution)/shard_map/all_to_all | solution.py:344
  19.4 0.7 copy-start.5
  20.1 0.6 copy-start.7
  53.8 1.0 copy-start.3
  54.8 15.0 %copy-start.4 = (bf16[2,256,256]{2,1,0:T(8,128)(2,1)S(1)}, bf16[2,256,256]{2,1,0:T(8,128)(2,1)}, u32[]{:S(2)}) copy-start(bf16[2,256,256]{2,1,0:T(8,128)(2,1)} %constant.65.clone.high_ref) | copy-start | bytes 786436
  54.8 15.0 %copy-start.6 = (f32[8,8,512]{2,1,0:T(8,128)S(1)}, f32[8,8,512]{2,1,0:T(8,128)}, u32[]{:S(2)}) copy-start(f32[8,8,512]{2,1,0:T(8,128)} %copy-done.5) | copy-start | bytes 393220
  54.8 15.0 %copy-start.8 = (f32[2,8,512]{2,1,0:T(8,128)S(1)}, f32[2,8,512]{2,1,0:T(8,128)}, u32[]{:S(2)}) copy-start(f32[2,8,512]{2,1,0:T(8,128)} %copy-done.7) | copy-start | bytes 98308
  73.5 45.8 %copy-start = (bf16[2,256,256]{2,1,0:T(8,128)(2,1)S(1)}, bf16[2,256,256]{2,1,0:T(8,128)(2,1)}, u32[]{:S(2)}) copy-start(bf16[2,256,256]{2,1,0:T(8,128)(2,1)} %constant.64.clone.low_ref) | copy-start | bytes 786436
  73.5 45.8 %copy-start.1 = (bf16[2,256,256]{2,1,0:T(8,128)(2,1)S(1)}, bf16[2,256,256]{2,1,0:T(8,128)(2,1)}, u32[]{:S(2)}) copy-start(bf16[2,256,256]{2,1,0:T(8,128)(2,1)} %constant.63.clone.high_ref) | copy-start | bytes 786436

commit v2 on v1

v2 whole, which is shorter than its diff:
```python
import math

import jax
import jax.numpy as jnp
import ml_dtypes
import numpy as np
from jax import lax
from jax.experimental import pallas as pl
from jax.experimental.pallas import tpu as pltpu
from jax.sharding import PartitionSpec as P

stream_weight = 0.04
span_weight = 0.16
shift_value = 0.0002


def split_table(values):
    high = values.astype(ml_dtypes.bfloat16)
    low = (values - high.astype(np.float64)).astype(ml_dtypes.bfloat16)
    return jnp.asarray(np.stack([high, low]))


def stream_table(nx_len):
    half = nx_len // 2
    wave = 2 * np.arange(half // 2)[None, None, :] + np.arange(2)[:, None, None]
    angle = 2.0 * math.pi / nx_len * (np.arange(half)[None, :, None] * wave % nx_len)
    return split_table(np.concatenate([np.cos(angle), -np.sin(angle)], axis=2))


def span_waves(nz_len):
    half = nz_len // 2
    wave = np.arange(half)
    return np.concatenate([wave, np.where(wave == 0, half, wave)])


def span_basis(points, nz_len):
    angle = 2.0 * math.pi / nz_len * (points[:, None] * span_waves(nz_len)[None, :] % nz_len)
    cosine = np.arange(nz_len)[None, :] <= nz_len // 2
    return np.where(cosine, np.cos(angle), np.sin(angle))


def plane_table(nz_len, groups):
    span = nz_len // groups
    block = np.arange(groups) * span
    return split_table(span_basis(np.concatenate([block - 1, block + span]) % nz_len, nz_len))


def cell_table(nz_len, groups):
    return split_table(span_basis(np.arange(nz_len).reshape(groups, -1).T.reshape(-1), nz_len))


def sine_matrix(span):
    index = np.arange(1, span + 1)
    return np.sin(math.pi / (span + 1) * index[:, None] * index[None, :])


def edge_table(span, some, steps):
    sines = sine_matrix(span) * (2.0 / (span + 1))
    eye = np.eye(some)
    table = np.zeros((steps, 2 * some + span, some * span))
    for chunk in range(steps):
        table[chunk, :some] = np.kron(eye, sines[:1])
        table[chunk, some : 2 * some] = np.kron(eye, sines[-1:])
    table[0, 2 * some :, :span] = sines
    table[-1, 2 * some :, -span:] = sines
    return split_table(table)


def halves(values):
    high = values.astype(jnp.bfloat16)
    low = (values - high.astype(jnp.float32)).astype(jnp.bfloat16)
    return high, low


def dot3(a, b, dims):
    def one(left, right):
        return lax.dot_general(left, right, (dims, ((), ())), preferred_element_type=jnp.float32)

    return one(a[0], b[0]) + (one(a[0], b[1]) + one(a[1], b[0]))


def swap_bits(tiles):
    tiles = list(tiles)
    lanes = tiles[0].shape[1]
    lane = lax.broadcasted_iota(jnp.int32, tiles[0].shape, 1)
    bit = len(tiles) // 2
    while bit:
        upper = (lane & bit) != 0
        for first in range(len(tiles)):
            if first & bit:
                continue
            a, b = tiles[first], tiles[first | bit]
            tiles[first] = jnp.where(upper, pltpu.roll(b, bit, 1), a)
            tiles[first | bit] = jnp.where(upper, b, pltpu.roll(a, lanes - bit, 1))
        bit //= 2
    return tiles


def turn(value, shift):
    lanes = value.shape[1]
    return value if shift % lanes == 0 else pltpu.roll(value, shift % lanes, 1)


def both(values):
    return jnp.concatenate([values, values], axis=0)


def wide(values):
    half = values.shape[1] // 2
    low, high = values[:, :half], values[:, half:]
    return jnp.concatenate([low, low, high, high], axis=1)


def local_forward(place_ref, lower_ref, upper_ref, sigma_ref, rhs_ref, stream_ref, sine_ref, edge_ref, rows_ref, inv_ref, send_ref, sol_ref, edges_ref):
    rows, span, nx_len = rows_ref.shape
    some = rhs_ref.shape[0]
    half = nx_len // 2
    index = pl.program_id(0)
    steps = rows // some
    field = rhs_ref[...].reshape(some * span, nx_len)
    first, second = field[:, :half], field[:, half:]
    parts = []
    for parity, folded in enumerate((first + second, first - second)):
        parts.append(dot3(halves(folded), (stream_ref[0, parity], stream_ref[1, parity]), ((1,), (0,))))
    lane = lax.broadcasted_iota(jnp.int32, (1, nx_len), 1)
    scale = jnp.where(lane == 0, 1.0 / nx_len, 2.0 / nx_len)
    modes = jnp.concatenate(parts, axis=1) * scale
    modes = dot3((sine_ref[0], sine_ref[1]), halves(modes), ((1,), (0,)))
    rows_ref[pl.ds(index * some, some)] = modes.reshape(some, span, nx_len)

    @pl.when(index == steps - 1)
    def _():
        base = place_ref[1] * rows
        sigma = sigma_ref[...]
        step = 8

        def descend(chunk, carry):
            value, numer, denom = carry
            for k in range(step):
                row = chunk * step + k
                low, high = lower_ref[base + row], upper_ref[base + row]
                numer = low * numer + sigma * denom
                new = numer + high * denom
                inv = denom / new
                denom = new
                inv_ref[row] = inv
                value = (low * value - rows_ref[row]) * wide(inv)
                sol_ref[row] = value
            return value, numer, denom

        one = jnp.ones_like(sigma)
        zero = jnp.zeros((span, nx_len), jnp.float32)
        lax.fori_loop(0, rows // step, descend, (zero, one, one))

        def ascend(chunk, value):
            for k in range(step):
                row = rows - 1 - (chunk * step + k)
                value = sol_ref[row] + wide(upper_ref[base + row] * inv_ref[row]) * value
                sol_ref[row] = value
            return value

        lax.fori_loop(0, rows // step, ascend, zero)
        for chunk in range(steps):
            part = sol_ref[chunk * some : chunk * some + some].reshape(some * span, nx_len)
            edges = dot3((edge_ref[0, chunk], edge_ref[1, chunk]), halves(part), ((1,), (0,)))
            edges_ref[chunk * some : chunk * some + some] = edges[:some]
            edges_ref[rows + chunk * some : rows + chunk * some + some] = edges[some : 2 * some]
            if chunk == 0:
                edges_ref[2 * rows : 2 * rows + span] = edges[2 * some :]
            if chunk == steps - 1:
                edges_ref[2 * rows + span :] = edges[2 * some :]
        groups, both_parts, _ = send_ref.shape
        count = both_parts // 2
        quarter = nx_len // 4
        for tile in range(4):
            turned = edges_ref[:, tile * quarter : tile * quarter + quarter].T
            place = tile // 2 * (groups // 2)
            part = tile % 2 * count
            send_ref[place : place + groups // 2, part : part + count] = turned.reshape(groups // 2, count, -1)


def local_inverse(place_ref, lower_ref, upper_ref, piece_ref, rows_ref, inv_ref, weight_ref, stream_ref, sine_ref, out_ref, sol_ref, edges_ref):
    rows, span, nx_len = rows_ref.shape
    some = out_ref.shape[0]
    half = nx_len // 2
    index = pl.program_id(0)

    @pl.when(index == 0)
    def _():
        base = place_ref[1] * rows
        groups, both_parts, _ = piece_ref.shape
        count = both_parts // 2
        quarter = nx_len // 4
        for tile in range(4):
            place = tile // 2 * (groups // 2)
            part = tile % 2 * count
            block = piece_ref[place : place + groups // 2, part : part + count]
            edges_ref[:, tile * quarter : tile * quarter + quarter] = block.reshape(quarter, -1).T
        sines = (sine_ref[0, :span, :span], sine_ref[1, :span, :span])
        before = dot3(sines, halves(edges_ref[2 * rows : 2 * rows + span]), ((1,), (0,)))
        after = dot3(sines, halves(edges_ref[2 * rows + span :]), ((1,), (0,)))
        weight_low, weight_high = weight_ref[0], weight_ref[1]
        step = 8

        def descend(chunk, value):
            for k in range(step):
                row = chunk * step + k
                source = rows_ref[row] - weight_low * edges_ref[pl.ds(row, 1)] - weight_high * edges_ref[pl.ds(rows + row, 1)]
                value = (lower_ref[base + row] * value - source) * wide(inv_ref[row])
                sol_ref[row] = value
            return value

        lax.fori_loop(0, rows // step, descend, before)

        def ascend(chunk, value):
            for k in range(step):
                row = rows - 1 - (chunk * step + k)
                value = sol_ref[row] + wide(upper_ref[base + row] * inv_ref[row]) * value
                sol_ref[row] = value
            return value

        lax.fori_loop(0, rows // step, ascend, after)

    modes = sol_ref[pl.ds(index * some, some)].reshape(some * span, nx_len)
    field = dot3((sine_ref[0], sine_ref[1]), halves(modes), ((1,), (0,))) * (2.0 / (span + 1))
    outs = []
    for parity in range(2):
        part = field[:, parity * half : parity * half + half]
        outs.append(dot3(halves(part), (stream_ref[0, parity], stream_ref[1, parity]), ((1,), (1,))))
    even, odd = outs
    out_ref[:, :, :half] = (even + odd).reshape(some, span, half)
    out_ref[:, :, half:] = (even - odd).reshape(some, span, half)


def factor(place_ref, lower_ref, upper_ref, waves_ref, both_ref, carry_down_ref, carry_up_ref, close_ref, start_ref):
    rows = both_ref.shape[1]
    blocks = carry_down_ref.shape[0]
    total = rows * blocks
    sigma = waves_ref[...]
    one = jnp.ones_like(sigma)
    step = 8

    def step_down(row, numer, denom):
        numer = lower_ref[row] * numer + sigma * denom
        return numer, numer + upper_ref[row] * denom

    def step_up(row, numer, denom):
        numer = upper_ref[row] * numer + sigma * denom
        return numer, numer + lower_ref[row] * denom

    def block(index, carry):
        t_down, t_up = carry
        other = blocks - 1 - index
        start_ref[0, index] = t_down
        start_ref[1, other] = t_up

        def some(chunk, inner):
            nd, dd, nu, du, prod_l, prod_u = inner
            for k in range(step):
                row = index * rows + chunk * step + k
                back = total - 1 - row
                nd, dd = step_down(row, nd, dd)
                nu, du = step_up(back, nu, du)
                prod_l = prod_l * lower_ref[row]
                prod_u = prod_u * upper_ref[back]
            return nd, dd, nu, du, prod_l, prod_u

        unit = jnp.float32(1.0)
        nd, dd, nu, du, prod_l, prod_u = lax.fori_loop(
            0, rows // step, some, (t_down, one, t_up, one, unit, unit)
        )
        inv_d = 1.0 / dd
        inv_u = 1.0 / du
        carry_down_ref[index] = prod_l * inv_d
        carry_up_ref[other] = prod_u * inv_u
        return nd * inv_d, nu * inv_u

    lax.fori_loop(0, blocks, block, (one, one))
    place = place_ref[1]
    first = place * rows

    def own(chunk, inner):
        nd, dd, nu, du = inner
        for k in range(step):
            row = chunk * step + k
            back = rows - 1 - row
            nd, new_d = step_down(first + row, nd, dd)
            both_ref[0, row] = dd / new_d
            nu, new_u = step_up(first + back, nu, du)
            both_ref[1, back] = du / new_u
            dd, du = new_d, new_u
        return nd, dd, nu, du

    nd, dd, nu, du = lax.fori_loop(
        0, rows // step, own, (start_ref[0, place], one, start_ref[1, place], one)
    )
    t_end = nd / dd
    t_next = start_ref[1, place]
    is_last = place == blocks - 1
    inner = jnp.where(is_last, 0.0, 1.0 / (t_next + t_end * (1.0 - t_next)))
    close_ref[0] = inner
    close_ref[1] = inner * (1.0 - t_next)
    close_ref[2] = 1.0 - start_ref[0, place]
    close_ref[3] = 1.0 - t_next


def span_forward(place_ref, lower_ref, upper_ref, piece_ref, factor_ref, close_ref, plane_ref, cell_ref, rows_ref, send_ref, keep_ref, edge_ref):
    groups, parts, lanes = piece_ref.shape
    rows, _, nz_len = rows_ref.shape
    span = nz_len // groups
    per = lanes // groups
    tiles = swap_bits([piece_ref[t] for t in range(groups)])
    lane = lax.broadcasted_iota(jnp.int32, (parts, lanes), 1)

    def source(value, group):
        return turn(tiles[value % groups], groups * (group - value // groups))

    for row in range(rows):
        pair = jnp.where(lane < groups, source(row, 0), source(rows + row, 1))
        keep_ref[row] = jnp.where(lane < 2 * groups, pair, 0.0)
    wave = lax.broadcasted_iota(jnp.int32, (1, nz_len), 1)
    scale = jnp.where(wave % (nz_len // 2) == 0, 1.0 / nz_len, 2.0 / nz_len)
    planes = keep_ref[...].reshape(rows * parts, lanes)
    spec = dot3(halves(planes), (plane_ref[0], plane_ref[1]), ((1,), (0,)))
    rows_ref[...] = (spec * (-span_weight * scale)).reshape(rows, parts, nz_len)
    cells = []
    for side in range(2):
        built = []
        for tile in range(nz_len // lanes):
            value = source(2 * rows + side * span + tile * per, 0)
            for group in range(1, per):
                other = source(2 * rows + side * span + tile * per + group, group)
                value = jnp.where(lane < groups * group, value, other)
            built.append(value)
        cells.append(jnp.concatenate(built, axis=1))
    edges = dot3(halves(jnp.concatenate(cells, axis=0)), (cell_ref[0], cell_ref[1]), ((1,), (0,))) * scale
    low_edge, high_edge = edges[:parts], edges[parts:]
    edge_ref[0] = low_edge
    edge_ref[1] = high_edge
    base = place_ref[1] * rows
    step = 8

    def sweep(chunk, carry):
        down, up = carry
        for k in range(step):
            row = chunk * step + k
            back = rows - 1 - row
            down = (lower_ref[base + row] * down - rows_ref[row]) * both(factor_ref[0, row])
            up = (upper_ref[base + back] * up - rows_ref[back]) * both(factor_ref[1, back])
        return down, up

    start = (both(close_ref[2]) * low_edge, both(close_ref[3]) * high_edge)
    down, up = lax.fori_loop(0, rows // step, sweep, start)
    down = down + high_edge
    up = up + low_edge
    for target in range(send_ref.shape[0]):
        send_ref[target] = jnp.where(target > place_ref[1], down, up)


def span_inverse(place_ref, lower_ref, upper_ref, rows_ref, ends_ref, keep_ref, edge_ref, factor_ref, carry_down_ref, carry_up_ref, close_ref, plane_ref, cell_ref, out_ref, grow_ref, near_ref):
    groups, parts, lanes = out_ref.shape
    rows, _, nz_len = rows_ref.shape
    blocks = ends_ref.shape[0]
    span = nz_len // groups
    per = lanes // groups
    place = place_ref[1]
    base = place * rows
    step = 8
    zero = jnp.zeros((parts, nz_len), jnp.float32)
    before = lax.fori_loop(
        0, place, lambda k, value: ends_ref[k] + both(carry_down_ref[k]) * value, zero
    )

    def climb(k, value):
        other = blocks - 1 - k
        return ends_ref[other] + both(carry_up_ref[other]) * value

    after = lax.fori_loop(0, blocks - 1 - place, climb, zero)
    before = before + both(close_ref[2]) * edge_ref[0]
    after = after + both(close_ref[3]) * edge_ref[1]

    def descend(chunk, value):
        for k in range(step):
            row = chunk * step + k
            value = (lower_ref[base + row] * value - rows_ref[row]) * both(factor_ref[0, row])
            grow_ref[row] = value
        return value

    last = lax.fori_loop(0, rows // step, descend, before)
    beyond = both(close_ref[0]) * after + both(close_ref[1]) * last

    def ascend(chunk, value):
        for k in range(step):
            row = rows - 1 - (chunk * step + k)
            ratio = upper_ref[base + row] * factor_ref[0, row]
            value = grow_ref[row] + both(ratio) * value
            grow_ref[row] = value
        return value

    first = lax.fori_loop(0, rows // step, ascend, beyond)
    below = before + both(close_ref[2]) * first
    flat = grow_ref[...].reshape(rows * parts, nz_len)
    near = dot3(halves(flat), (plane_ref[0], plane_ref[1]), ((1,), (1,)))
    near_ref[...] = near.reshape(rows, parts, lanes)
    edges = jnp.concatenate([below, beyond], axis=0)
    cells = dot3(halves(edges), (cell_ref[0], cell_ref[1]), ((1,), (1,)))
    lane = lax.broadcasted_iota(jnp.int32, (parts, lanes), 1)
    total = []
    for row in range(rows):
        own = keep_ref[row]
        left = jnp.where(lane == 0, turn(own, 1 - 2 * groups), turn(own, 1 - groups))
        right = jnp.where(lane == 2 * groups - 1, turn(own, 2 * groups - 1), turn(own, groups - 1))
        total.append(near_ref[row] + jnp.where(lane < groups, left, right))

    def piece(value, group):
        if value < rows:
            return turn(total[value], groups * group)
        if value < 2 * rows:
            return turn(total[value - rows], groups * (group - 1))
        side, cell = divmod(value - 2 * rows, span)
        tile, part = divmod(cell, per)
        found = cells[side * parts : side * parts + parts, tile * lanes : tile * lanes + lanes]
        return turn(found, groups * (group - part))

    tiles = []
    for t in range(groups):
        value = piece(t, 0)
        for group in range(1, per):
            value = jnp.where(lane < groups * group, value, piece(groups * group + t, group))
        tiles.append(value)
    for t, value in enumerate(swap_bits(tiles)):
        out_ref[t] = value


smem = pl.BlockSpec(memory_space=pltpu.SMEM)
vmem = pl.BlockSpec(memory_space=pltpu.VMEM)


def local(rhs, lower, upper):
    rows, span, nx_len = rhs.shape
    groups = lax.axis_size("row")
    blocks = lax.axis_size("col")
    nz_len = span * groups
    modes = nx_len // 2 // groups
    parts = 2 * modes
    steps = 3
    some = rows // steps
    lanes = 2 * (rows + span)
    place = jnp.stack([lax.axis_index("row"), lax.axis_index("col")]).astype(jnp.int32)
    f32 = jnp.float32
    params = pltpu.CompilerParams(vmem_limit_bytes=40 * 1024 * 1024)
    stream = stream_table(nx_len)
    sines = split_table(np.kron(np.eye(some), sine_matrix(span)))
    edge = edge_table(span, some, steps)
    plane = plane_table(nz_len, groups)
    plane = jnp.pad(plane, ((0, 0), (0, lanes - 2 * groups), (0, 0)))
    cell = cell_table(nz_len, groups)
    ends_of_block = sine_matrix(span)[[0, -1]] * span_weight
    weights = jnp.asarray(np.broadcast_to(ends_of_block[:, :, None], (2, span, nx_len)).astype(np.float32))

    def on_chip(*shape):
        return pltpu.VMEM(shape, f32)

    def on_hbm(value):
        return pltpu.with_memory_space_constraint(value, pltpu.HBM)

    def exchange(value, axis):
        return lax.all_to_all(value, axis, split_axis=0, concat_axis=0, tiled=True)

    def stream_part(index):
        angle = 2.0 * math.pi / nx_len * index.astype(f32)
        return stream_weight * (2.0 - 2.0 * jnp.cos(angle))

    def span_part(index, count):
        angle = 2.0 * math.pi / count * index.astype(f32)
        return span_weight * (2.0 - 2.0 * jnp.cos(angle))

    quarter = nx_len // 4
    every = jnp.arange(nx_len // 2)
    kx = 2 * (every % quarter) + every // quarter
    kz = span_part(jnp.arange(1, span + 1), 2 * (span + 1))
    sigma_own = kz[:, None] + stream_part(kx)[None, :] + shift_value
    field_spec = pl.BlockSpec((some, span, nx_len), lambda i: (i, 0, 0))
    own_rows, own_inv, send = pl.pallas_call(
        local_forward,
        grid=(steps,),
        in_specs=[smem, smem, smem, vmem, field_spec, vmem, vmem, vmem],
        out_specs=[vmem] * 3,
        out_shape=[on_chip(rows, span, nx_len), on_chip(rows, span, nx_len // 2), on_chip(groups, parts, lanes)],
        scratch_shapes=[on_chip(rows, span, nx_len), on_chip(lanes, nx_len)],
        compiler_params=params,
        name="local_forward",
    )(place, lower, upper, sigma_own, on_hbm(rhs), stream, sines, edge)
    piece = exchange(send, "row")

    order = place[0] * modes + jnp.arange(modes)
    kx = 2 * (order % quarter) + order // quarter
    kz = jnp.asarray(span_waves(nz_len).astype(np.int32))
    sigma = stream_part(kx)[:, None] + span_part(kz, nz_len)[None, :] + shift_value
    factors, carry_down, carry_up, close = pl.pallas_call(
        factor,
        in_specs=[smem, smem, smem, vmem],
        out_specs=[vmem] * 4,
        out_shape=[
            on_chip(2, rows, modes, nz_len),
            on_chip(blocks, modes, nz_len),
            on_chip(blocks, modes, nz_len),
            on_chip(4, modes, nz_len),
        ],
        scratch_shapes=[on_chip(2, blocks, modes, nz_len)],
        compiler_params=params,
        name="factor",
    )(place, lower, upper, sigma)

    mode_rows, ends, keep, edges = pl.pallas_call(
        span_forward,
        in_specs=[smem, smem, smem] + [vmem] * 5,
        out_specs=[vmem] * 4,
        out_shape=[
            on_chip(rows, parts, nz_len),
            on_chip(blocks, parts, nz_len),
            on_chip(rows, parts, lanes),
            on_chip(2, parts, nz_len),
        ],
        compiler_params=params,
        name="span_forward",
    )(place, lower, upper, piece, factors, close, plane, cell)
    ends = exchange(ends, "col")

    send = pl.pallas_call(
        span_inverse,
        in_specs=[smem, smem, smem] + [vmem] * 10,
        out_specs=vmem,
        out_shape=on_chip(groups, parts, lanes),
        scratch_shapes=[on_chip(rows, parts, nz_len), on_chip(rows, parts, lanes)],
        compiler_params=params,
        name="span_inverse",
    )(place, lower, upper, mode_rows, ends, keep, edges, factors, carry_down, carry_up, close, plane, cell)
    piece = exchange(send, "row")

    return pl.pallas_call(
        local_inverse,
        grid=(steps,),
        in_specs=[smem, smem, smem] + [vmem] * 6,
        out_specs=field_spec,
        out_shape=jax.ShapeDtypeStruct((rows, span, nx_len), f32),
        scratch_shapes=[on_chip(rows, span, nx_len), on_chip(lanes, nx_len)],
        compiler_params=params,
        name="local_inverse",
    )(place, lower, upper, piece, own_rows, own_inv, weights, stream, sines)


def solution(mesh):
    return jax.shard_map(
        local,
        mesh=mesh,
        in_specs=(P("col", "row", None), P(), P()),
        out_specs=P("col", "row", None),
        check_vma=False,
    )
```

time: 122 us -> 73.8 us (0.60)
  blocking collectives: 57.6 us -> 27.9 us
  waiting for transfers between devices: 33.1 us -> 8.24 us
  local copies, waits for them, and re-layouts: 2.24 us -> 6.4 us
  Pallas kernels: 17.3 us -> 19.2 us
    all_to_all x2, blocking collectives: 57.6 us -> 27.9 us  [exchange(): return lax.all_to_all(value, axis, split_axis=0, concat_axis=0, tiled=True)]
    all_to_all x1, waiting for transfers between devices: 33.1 us -> 8.24 us  [exchange(): return lax.all_to_all(value, axis, split_axis=0, concat_axis=0, tiled=True)]
    unnamed x24 -> x34, local copies, waits for them, and re-layouts: 2.24 us -> 6.4 us
    pallas_call x4, Pallas kernels: 13.5 us -> 15.4 us  [the longest x1 5.64 us: local(): pl.pallas_call(local_forward, grid=(steps,), in_specs=[smem, smem, smem,...]
  transfers between devices with their start and end apart: 1 -> 1, of which waited for: 1 -> 1; matrix products, arithmetic and copies ran while one was open for 0% -> 0% of each run, Pallas kernels for 3% -> 5%
where the time goes in v2:
time: 73.8 us; the launch traced here: 73.4 us
  blocking collectives  27.9 us (38%)
  Pallas kernels  19.2 us (26%)
  starting transfers between devices  11.2 us (15%)
  waiting for transfers between devices  8.24 us (11%)
  local copies, waits for them, and re-layouts  6.4 us (9%)
    all_to_all x2, blocking collectives, exchange(): return lax.all_to_all(value, axis, split_axis=0, concat_axis=0, tiled=True)  27.9 us
    all_to_all x1, starting transfers between devices, exchange(): return lax.all_to_all(value, axis, split_axis=0, concat_axis=0, tiled=True)  11.2 us
    all_to_all x1, waiting for transfers between devices, exchange(): return lax.all_to_all(value, axis, split_axis=0, concat_axis=0, tiled=True)  8.24 us
    unnamed x34, local copies, waits for them, and re-layouts  6.4 us
    pallas_call x1, Pallas kernels, local(): pl.pallas_call(local_forward, grid=(steps,), in_specs=[smem, smem, smem,...  5.64 us
    pallas_call x1, Pallas kernels, local(): pl.pallas_call(local_inverse, grid=(steps,), in_specs=[smem, smem, smem]...  4.54 us
    pallas_call x1, Pallas kernels, local(): pl.pallas_call(factor, in_specs=[smem, smem, smem, vmem], out_specs=[vmem...  3.77 us
    pallas_call x1, Pallas kernels, local(): pl.pallas_call(span_inverse, in_specs=[smem, smem, smem] + [vmem] * 10, o...  2.83 us
  transfers between devices with their start and end apart: 1, of which 1 were waited for; matrix products, arithmetic and copies ran while one was open for 0% of the time, Pallas kernels for 5%

profile of v2, /device:TPU:32, one launch (start us, length us, event | category | flops | bytes accessed | tf_op | source)
XLA Modules:
  0.0 73.4 jit_solution(5017126787374053600)
XLA Ops:
  0.0 0.0 copy-start.16
  0.0 0.0 copy-start
  0.1 0.1 pad_add_fusion.place_ref
  0.2 0.1 add_add_fusion.1.sigma_ref
  0.3 0.0 copy-start.1
  0.3 1.1 %copy-done.1 = bf16[2,2,256,256]{3,2,1,0:T(8,128)(2,1)S(1)} copy-done((bf16[2,2,256,256]{3,2,1,0:T(8,128)(2,1)S(1)}, bf16[2,2,256,256]{3,2,1,0:T(8,128)(2,1)}, u32[]{:S(2)}) %copy-start.1) | copy-done | bytes 524312
  1.4 0.0 copy-start.5
  1.4 0.9 %copy-done.5 = bf16[2,256,256]{2,1,0:T(8,128)(2,1)S(1)} copy-done((bf16[2,256,256]{2,1,0:T(8,128)(2,1)S(1)}, bf16[2,256,256]{2,1,0:T(8,128)(2,1)}, u32[]{:S(2)}) %copy-start.5) | copy-done | bytes 262168
  2.3 0.0 copy-start.10
  2.3 0.9 %copy-done.10 = bf16[2,3,48,256]{3,2,1,0:T(8,128)(2,1)S(1)} copy-done((bf16[2,3,48,256]{3,2,1,0:T(8,128)(2,1)S(1)}, bf16[2,3,48,256]{3,2,1,0:T(8,128)(2,1)}, u32[]{:S(2)}) %copy-start.10) | copy-done | bytes 147480
  3.2 0.0 copy-start.12
  3.2 0.7 copy-done.12
  3.9 0.0 copy-start.14
  3.9 0.7 copy-done.14
  4.6 0.0 copy-start.13
  4.6 0.0 copy-start.15
  4.6 0.0 copy-start.7
  4.6 5.6 %local_forward.1 = (f32[48,16,512]{2,1,0:T(8,128)S(1)}, f32[48,16,256]{2,1,0:T(8,128)S(1)}, f32[32,16,128]{2,1,0:T(8,128)}) custom-call(s32[2]{0:T(128)S(1)} %pad_add_fusion.place_ref, f32[384]{0:T(512)S(1)} %copy-done.12, f32[384]{0:T(512)S(1)} %copy-done.14, f32[16,256]{1,0:T(8,128)S(1)} %add_add_fusion.1.sigma_ref, f32[48,16,512]{2,1,0:T(8,128)} %rhs_ref.1, ...), custom_call_target="tpu_custom_call" | custom-call | tf_op jit(solution)/shard_map/local_forward/pallas_call | solution.py:484
  10.2 0.0 copy-start.3
  10.2 1.1 %copy-done.3 = f32[48,16,512]{2,1,0:T(8,128)} copy-done((f32[48,16,512]{2,1,0:T(8,128)}, f32[48,16,512]{2,1,0:T(8,128)S(1)}, u32[]{:S(2)}) %copy-start.3) | copy-done | bytes 1572888
  11.4 0.0 copy-start.8
  11.4 0.9 %copy-done.8 = f32[48,16,256]{2,1,0:T(8,128)} copy-done((f32[48,16,256]{2,1,0:T(8,128)}, f32[48,16,256]{2,1,0:T(8,128)S(1)}, u32[]{:S(2)}) %copy-start.8) | copy-done | bytes 786456
  12.3 11.2 %all-to-all-start = ((f32[32,16,128]{2,1,0:T(8,128)}), f32[32,16,128]{2,1,0:T(8,128)S(1)}, u32[]{:S(2)}, u32[]{:S(2)}) async-start(f32[32,16,128]{2,1,0:T(8,128)} %get-tuple-element.16), calls=%async_computation | async-start | bytes 524288 | tf_op jit(solution)/shard_map/all_to_all | solution.py:468
  23.5 0.1 subtract_multiply_fusion
  23.5 0.0 copy-done.16
  23.5 0.1 add_add_fusion.waves_ref
  23.6 0.0 copy-done.13
  23.6 0.0 copy-done.15
  23.6 3.8 %factor.1 = (f32[2,48,8,512]{3,2,1,0:T(8,128)S(1)}, f32[8,8,512]{2,1,0:T(8,128)S(1)}, f32[8,8,512]{2,1,0:T(8,128)S(1)}, f32[4,8,512]{2,1,0:T(8,128)S(1)}) custom-call(s32[2]{0:T(128)S(1)} %pad_add_fusion.place_ref, f32[384]{0:T(512)S(1)} %copy-done.13, f32[384]{0:T(512)S(1)} %copy-done.15, f32[8,512]{1,0:T(8,128)S(1)} %add_add_fusion.waves_ref), custom_call_target="tpu_custom_call" | custom-call | tf_op jit(solution)/shard_map/factor/pallas_call | solution.py:500
  27.4 8.2 %all-to-all-done.piece_ref = f32[32,16,128]{2,1,0:T(8,128)S(1)} async-done(((f32[32,16,128]{2,1,0:T(8,128)}), f32[32,16,128]{2,1,0:T(8,128)S(1)}, u32[]{:S(2)}, u32[]{:S(2)}) %all-to-all-start) | async-done | bytes 262176 | tf_op jit(solution)/shard_map/all_to_all | solution.py:468
  35.6 0.0 copy-done
  35.6 0.0 copy-done.7
  35.6 2.4 %span_forward.1 = (f32[48,16,512]{2,1,0:T(8,128)S(1)}, f32[8,16,512]{2,1,0:T(8,128)S(1)}, f32[48,16,128]{2,1,0:T(8,128)S(1)}, f32[2,16,512]{2,1,0:T(8,128)S(1)}) custom-call(s32[2]{0:T(128)S(1)} %pad_add_fusion.place_ref, f32[384]{0:T(512)S(1)} %copy-done.13, f32[384]{0:T(512)S(1)} %copy-done.15, f32[32,16,128]{2,1,0:T(8,128)S(1)} %all-to-all-done.piece_ref, ...), custom_call_target="tpu_custom_call" | custom-call | tf_op jit(solution)/shard_map/span_forward/pallas_call | solution.py:515
  38.0 11.8 %all_to_all.15.ends_ref = f32[8,16,512]{2,1,0:T(8,128)S(1)} all-to-all(f32[8,16,512]{2,1,0:T(8,128)S(1)} %get-tuple-element.20), channel_id=1, replica_groups=mesh['row'=32,'col'=8] {'col'}, dimensions={0} | all-to-all | bytes 524288 | tf_op jit(solution)/shard_map/all_to_all | solution.py:468
  49.8 0.0 copy-start.2
  49.8 0.0 copy-start.4
  49.8 0.0 copy-start.6
  49.8 0.0 copy-start.9
  49.8 0.0 copy-start.11
  49.8 2.8 %span_inverse.1 = f32[32,16,128]{2,1,0:T(8,128)S(1)} custom-call(s32[2]{0:T(128)S(1)} %pad_add_fusion.place_ref, f32[384]{0:T(512)S(1)} %copy-done.13, f32[384]{0:T(512)S(1)} %copy-done.15, f32[48,16,512]{2,1,0:T(8,128)S(1)} %get-tuple-element.19.rows_ref, f32[8,16,512]{2,1,0:T(8,128)S(1)} %all_to_all.15.ends_ref, ...), custom_call_target="tpu_custom_call" | custom-call | tf_op jit(solution)/shard_map/span_inverse/pallas_call | solution.py:530
  52.7 16.2 %all_to_all.16.piece_ref = f32[32,16,128]{2,1,0:T(8,128)S(1)} all-to-all(f32[32,16,128]{2,1,0:T(8,128)S(1)} %span_inverse.1), channel_id=1, replica_groups=mesh['row'=32,'col'=8] {'row'}, dimensions={0} | all-to-all | bytes 524288 | tf_op jit(solution)/shard_map/all_to_all | solution.py:468
  68.8 0.0 copy-done.2
  68.8 0.0 copy-done.4
  68.8 0.0 copy-done.6
  68.8 0.0 copy-done.9
  68.8 0.0 copy-done.11
  68.9 4.5 %local_inverse.1 = f32[48,16,512]{2,1,0:T(8,128)} custom-call(s32[2]{0:T(128)S(1)} %pad_add_fusion.place_ref, f32[384]{0:T(512)S(1)} %copy-done.13, f32[384]{0:T(512)S(1)} %copy-done.15, f32[32,16,128]{2,1,0:T(8,128)S(1)} %all_to_all.16.piece_ref, f32[48,16,512]{2,1,0:T(8,128)S(1)} %copy-done.4, f32[48,16,256]{2,1,0:T(8,128)S(1)} %copy-done.9, ...), custom_call_target="tpu_custom_call" | custom-call | tf_op jit(solution)/shard_map/local_inverse/pallas_call | solution.py:541
  (2 shorter events, 0.1 us)
Async XLA Ops:
  0.0 23.5 %copy-start.16 = (f32[512]{0:T(512)S(1)}, f32[512]{0:T(512)}, u32[]{:S(2)}) copy-start(f32[512]{0:T(512)} %constant.115) | copy-start | bytes 6148
  0.0 35.6 %copy-start = (bf16[2,512,512]{2,1,0:T(8,128)(2,1)S(1)}, bf16[2,512,512]{2,1,0:T(8,128)(2,1)}, u32[]{:S(2)}) copy-start(bf16[2,512,512]{2,1,0:T(8,128)(2,1)} %constant.104.clone.cell_ref) | copy-start | bytes 3145732
  0.3 1.1 %copy-start.1 = (bf16[2,2,256,256]{3,2,1,0:T(8,128)(2,1)S(1)}, bf16[2,2,256,256]{3,2,1,0:T(8,128)(2,1)}, u32[]{:S(2)}) copy-start(bf16[2,2,256,256]{3,2,1,0:T(8,128)(2,1)} %constant.100.clone.stream_ref) | copy-start | bytes 1572868
  1.4 0.9 %copy-start.5 = (bf16[2,256,256]{2,1,0:T(8,128)(2,1)S(1)}, bf16[2,256,256]{2,1,0:T(8,128)(2,1)}, u32[]{:S(2)}) copy-start(bf16[2,256,256]{2,1,0:T(8,128)(2,1)} %constant.101.clone.sine_ref) | copy-start | bytes 786436
  2.3 0.9 %copy-start.10 = (bf16[2,3,48,256]{3,2,1,0:T(8,128)(2,1)S(1)}, bf16[2,3,48,256]{3,2,1,0:T(8,128)(2,1)}, u32[]{:S(2)}) copy-start(bf16[2,3,48,256]{3,2,1,0:T(8,128)(2,1)} %constant.102.clone.edge_ref) | copy-start | bytes 442372
  3.2 0.7 copy-start.12
  3.9 0.7 copy-start.14
  4.6 19.0 %copy-start.13 = (f32[384]{0:T(512)S(1)}, f32[384]{0:T(512)}, u32[]{:S(2)}) copy-start(f32[384]{0:T(512)} %lower_ref.9) | copy-start | bytes 4612
  4.6 19.0 %copy-start.15 = (f32[384]{0:T(512)S(1)}, f32[384]{0:T(512)}, u32[]{:S(2)}) copy-start(f32[384]{0:T(512)} %upper_ref.9) | copy-start | bytes 4612
  4.6 31.0 %copy-start.7 = (bf16[2,128,512]{2,1,0:T(8,128)(2,1)S(1)}, bf16[2,128,512]{2,1,0:T(8,128)(2,1)}, u32[]{:S(2)}) copy-start(bf16[2,128,512]{2,1,0:T(8,128)(2,1)} %constant.116.plane_ref) | copy-start | bytes 786436
  10.2 1.1 %copy-start.3 = (f32[48,16,512]{2,1,0:T(8,128)}, f32[48,16,512]{2,1,0:T(8,128)S(1)}, u32[]{:S(2)}) copy-start(f32[48,16,512]{2,1,0:T(8,128)S(1)} %get-tuple-element.25.rows_ref) | copy-start | bytes 4718596
  11.4 0.9 %copy-start.8 = (f32[48,16,256]{2,1,0:T(8,128)}, f32[48,16,256]{2,1,0:T(8,128)S(1)}, u32[]{:S(2)}) copy-start(f32[48,16,256]{2,1,0:T(8,128)S(1)} %get-tuple-element.26.inv_ref) | copy-start | bytes 2359300
  12.3 23.4 %all-to-all-start = ((f32[32,16,128]{2,1,0:T(8,128)}), f32[32,16,128]{2,1,0:T(8,128)S(1)}, u32[]{:S(2)}, u32[]{:S(2)}) async-start(f32[32,16,128]{2,1,0:T(8,128)} %get-tuple-element.16), calls=%async_computation | async-start | bytes 524288 | tf_op jit(solution)/shard_map/all_to_all | solution.py:468
  49.8 19.0 %copy-start.2 = (bf16[2,2,256,256]{3,2,1,0:T(8,128)(2,1)S(1)}, bf16[2,2,256,256]{3,2,1,0:T(8,128)(2,1)}, u32[]{:S(2)}) copy-start(bf16[2,2,256,256]{3,2,1,0:T(8,128)(2,1)} %constant.100.clone.stream_ref) | copy-start | bytes 1572868
  49.8 19.0 %copy-start.4 = (f32[48,16,512]{2,1,0:T(8,128)S(1)}, f32[48,16,512]{2,1,0:T(8,128)}, u32[]{:S(2)}) copy-start(f32[48,16,512]{2,1,0:T(8,128)} %copy-done.3) | copy-start | bytes 4718596
  49.8 19.0 %copy-start.6 = (bf16[2,256,256]{2,1,0:T(8,128)(2,1)S(1)}, bf16[2,256,256]{2,1,0:T(8,128)(2,1)}, u32[]{:S(2)}) copy-start(bf16[2,256,256]{2,1,0:T(8,128)(2,1)} %constant.101.clone.sine_ref) | copy-start | bytes 786436
  49.8 19.0 %copy-start.9 = (f32[48,16,256]{2,1,0:T(8,128)S(1)}, f32[48,16,256]{2,1,0:T(8,128)}, u32[]{:S(2)}) copy-start(f32[48,16,256]{2,1,0:T(8,128)} %copy-done.8) | copy-start | bytes 2359300
  49.8 19.0 %copy-start.11 = (f32[2,16,512]{2,1,0:T(8,128)S(1)}, f32[2,16,512]{2,1,0:T(8,128)}, u32[]{:S(2)}) copy-start(f32[2,16,512]{2,1,0:T(8,128)} %constant.105.clone.weight_ref) | copy-start | bytes 196612

commit v3 on v2

--- a/solution.py
+++ b/solution.py
@@ -52,18 +52,6 @@
 def sine_matrix(span):
     index = np.arange(1, span + 1)
     return np.sin(math.pi / (span + 1) * index[:, None] * index[None, :])
-
-
-def edge_table(span, some, steps):
-    sines = sine_matrix(span) * (2.0 / (span + 1))
-    eye = np.eye(some)
-    table = np.zeros((steps, 2 * some + span, some * span))
-    for chunk in range(steps):
-        table[chunk, :some] = np.kron(eye, sines[:1])
-        table[chunk, some : 2 * some] = np.kron(eye, sines[-1:])
-    table[0, 2 * some :, :span] = sines
-    table[-1, 2 * some :, -span:] = sines
-    return split_table(table)
 
 
 def halves(values):
@@ -111,12 +99,18 @@
     return jnp.concatenate([low, low, high, high], axis=1)
 
 
-def local_forward(place_ref, lower_ref, upper_ref, sigma_ref, rhs_ref, stream_ref, sine_ref, edge_ref, rows_ref, inv_ref, send_ref, sol_ref, edges_ref):
-    rows, span, nx_len = rows_ref.shape
-    some = rhs_ref.shape[0]
+def local_forward(place_ref, lower_ref, upper_ref, sigma_ref, weight_ref, rhs_ref, stream_ref, sine_ref, rows_ref, inv_ref, send_ref, sol_ref, ratio_ref, value_ref, state_ref, edges_ref):
+    some, span, nx_len = rows_ref.shape
+    rows = sol_ref.shape[0]
     half = nx_len // 2
     index = pl.program_id(0)
     steps = rows // some
+
+    @pl.when(index == 0)
+    def _():
+        value_ref[...] = jnp.zeros_like(value_ref)
+        state_ref[...] = jnp.ones_like(state_ref)
+
     field = rhs_ref[...].reshape(some * span, nx_len)
     first, second = field[:, :half], field[:, half:]
     parts = []
@@ -126,49 +120,56 @@
     scale = jnp.where(lane == 0, 1.0 / nx_len, 2.0 / nx_len)
     modes = jnp.concatenate(parts, axis=1) * scale
     modes = dot3((sine_ref[0], sine_ref[1]), halves(modes), ((1,), (0,)))
-    rows_ref[pl.ds(index * some, some)] = modes.reshape(some, span, nx_len)
+    rows_ref[...] = modes.reshape(some, span, nx_len)
+    base = place_ref[1] * rows
+    sigma = sigma_ref[...]
+    step = 8
+
+    def descend(chunk, carry):
+        value, numer, denom = carry
+        for k in range(step):
+            row = chunk * step + k
+            cell = index * some + row
+            low, high = lower_ref[base + cell], upper_ref[base + cell]
+            numer = low * numer + sigma * denom
+            new = numer + high * denom
+            inv = denom / new
+            denom = new
+            inv_ref[row] = inv
+            ratio_ref[cell] = high * inv
+            value = (low * value - rows_ref[row]) * wide(inv)
+            sol_ref[cell] = value
+        return value, numer, denom
+
+    value, numer, denom = lax.fori_loop(
+        0, some // step, descend, (value_ref[...], state_ref[0], state_ref[1])
+    )
+    value_ref[...] = value
+    state_ref[0] = numer
+    state_ref[1] = denom
 
     @pl.when(index == steps - 1)
     def _():
-        base = place_ref[1] * rows
-        sigma = sigma_ref[...]
-        step = 8
-
-        def descend(chunk, carry):
-            value, numer, denom = carry
-            for k in range(step):
-                row = chunk * step + k
-                low, high = lower_ref[base + row], upper_ref[base + row]
-                numer = low * numer + sigma * denom
-                new = numer + high * denom
-                inv = denom / new
-                denom = new
-                inv_ref[row] = inv
-                value = (low * value - rows_ref[row]) * wide(inv)
-                sol_ref[row] = value
-            return value, numer, denom
-
-        one = jnp.ones_like(sigma)
-        zero = jnp.zeros((span, nx_len), jnp.float32)
-        lax.fori_loop(0, rows // step, descend, (zero, one, one))
+        weight = weight_ref[0] * (2.0 / ((span + 1) * span_weight))
+        flip = lax.broadcasted_iota(jnp.int32, (span // 2, nx_len), 0) % 2 == 0
 
         def ascend(chunk, value):
             for k in range(step):
                 row = rows - 1 - (chunk * step + k)
-                value = sol_ref[row] + wide(upper_ref[base + row] * inv_ref[row]) * value
+                value = sol_ref[row] + wide(ratio_ref[row]) * value
                 sol_ref[row] = value
+                part = weight * value
+                part = part[: span // 2] + part[span // 2 :]
+                edges_ref[pl.ds(row, 1)] = jnp.sum(part, axis=0, keepdims=True)
+                part = jnp.where(flip, part, -part)
+                edges_ref[pl.ds(rows + row, 1)] = jnp.sum(part, axis=0, keepdims=True)
             return value
 
-        lax.fori_loop(0, rows // step, ascend, zero)
-        for chunk in range(steps):
-            part = sol_ref[chunk * some : chunk * some + some].reshape(some * span, nx_len)
-            edges = dot3((edge_ref[0, chunk], edge_ref[1, chunk]), halves(part), ((1,), (0,)))
-            edges_ref[chunk * some : chunk * some + some] = edges[:some]
-            edges_ref[rows + chunk * some : rows + chunk * some + some] = edges[some : 2 * some]
-            if chunk == 0:
-                edges_ref[2 * rows : 2 * rows + span] = edges[2 * some :]
-            if chunk == steps - 1:
-                edges_ref[2 * rows + span :] = edges[2 * some :]
+        lax.fori_loop(0, rows // step, ascend, jnp.zeros((span, nx_len), jnp.float32))
+        sines = (sine_ref[0, :span, :span], sine_ref[1, :span, :span])
+        for side, row in enumerate((0, rows - 1)):
+            edge = dot3(sines, halves(sol_ref[row]), ((1,), (0,))) * (2.0 / (span + 1))
+            edges_ref[2 * rows + side * span : 2 * rows + side * span + span] = edge
         groups, both_parts, _ = send_ref.shape
         count = both_parts // 2
         quarter = nx_len // 4
@@ -451,7 +452,6 @@
     params = pltpu.CompilerParams(vmem_limit_bytes=40 * 1024 * 1024)
     stream = stream_table(nx_len)
     sines = split_table(np.kron(np.eye(some), sine_matrix(span)))
-    edge = edge_table(span, some, steps)
     plane = plane_table(nz_len, groups)
     plane = jnp.pad(plane, ((0, 0), (0, lanes - 2 * groups), (0, 0)))
     cell = cell_table(nz_len, groups)
@@ -463,6 +463,10 @@
 
     def on_hbm(value):
         return pltpu.with_memory_space_constraint(value, pltpu.HBM)
+
+    def fixed(value):
+        shape = value.shape
+        return pl.BlockSpec(shape, lambda i: (0,) * len(shape))
 
     def exchange(value, axis):
         return lax.all_to_all(value, axis, split_axis=0, concat_axis=0, tiled=True)
@@ -481,16 +485,28 @@
     kz = span_part(jnp.arange(1, span + 1), 2 * (span + 1))
     sigma_own = kz[:, None] + stream_part(kx)[None, :] + shift_value
     field_spec = pl.BlockSpec((some, span, nx_len), lambda i: (i, 0, 0))
+    mode_spec = pl.BlockSpec((some, span, nx_len), lambda i: (i, 0, 0))
+    inv_spec = pl.BlockSpec((some, span, nx_len // 2), lambda i: (i, 0, 0))
     own_rows, own_inv, send = pl.pallas_call(
         local_forward,
         grid=(steps,),
-        in_specs=[smem, smem, smem, vmem, field_spec, vmem, vmem, vmem],
-        out_specs=[vmem] * 3,
-        out_shape=[on_chip(rows, span, nx_len), on_chip(rows, span, nx_len // 2), on_chip(groups, parts, lanes)],
-        scratch_shapes=[on_chip(rows, span, nx_len), on_chip(lanes, nx_len)],
+        in_specs=[smem, smem, smem, vmem, fixed(weights), field_spec, fixed(stream), fixed(sines)],
+        out_specs=[mode_spec, inv_spec, vmem],
+        out_shape=[
+            pltpu.HBM((rows, span, nx_len), f32),
+            pltpu.HBM((rows, span, nx_len // 2), f32),
+            on_chip(groups, parts, lanes),
+        ],
+        scratch_shapes=[
+            on_chip(rows, span, nx_len),
+            on_chip(rows, span, nx_len // 2),
+            on_chip(span, nx_len),
+            on_chip(2, span, nx_len // 2),
+            on_chip(lanes, nx_len),
+        ],
         compiler_params=params,
         name="local_forward",
-    )(place, lower, upper, sigma_own, on_hbm(rhs), stream, sines, edge)
+    )(place, on_hbm(lower), on_hbm(upper), sigma_own, on_hbm(weights), on_hbm(rhs), on_hbm(stream), on_hbm(sines))
     piece = exchange(send, "row")
 
     order = place[0] * modes + jnp.arange(modes)

time: 73.8 us -> 68.2 us (0.924)
  local copies, waits for them, and re-layouts: 6.4 us -> 0.05 us
  Pallas kernels: 19.2 us -> 20 us
    unnamed x34 -> x20, local copies, waits for them, and re-layouts: 6.4 us -> 0.05 us
    pallas_call x1, Pallas kernels: 5.64 us -> 6.47 us  [local(): pl.pallas_call(local_forward, grid=(steps,), in_specs=[smem, smem, smem,...]
  transfers between devices with their start and end apart: 1 -> 1, of which waited for: 1 -> 1; matrix products, arithmetic and copies ran while one was open for 0% -> 0% of each run, Pallas kernels for 5% -> 6%
where the time goes in v3:
time: 68.2 us; the launch traced here: 67.9 us
  blocking collectives  27.9 us (41%)
  Pallas kernels  20 us (29%)
  starting transfers between devices  11.2 us (16%)
  waiting for transfers between devices  8.23 us (12%)
    all_to_all x2, blocking collectives, exchange(): return lax.all_to_all(value, axis, split_axis=0, concat_axis=0, tiled=True)  27.9 us
    all_to_all x1, starting transfers between devices, exchange(): return lax.all_to_all(value, axis, split_axis=0, concat_axis=0, tiled=True)  11.2 us
    all_to_all x1, waiting for transfers between devices, exchange(): return lax.all_to_all(value, axis, split_axis=0, concat_axis=0, tiled=True)  8.23 us
    pallas_call x1, Pallas kernels, local(): pl.pallas_call(local_forward, grid=(steps,), in_specs=[smem, smem, smem,...  6.47 us
    pallas_call x1, Pallas kernels, local(): pl.pallas_call(local_inverse, grid=(steps,), in_specs=[smem, smem, smem]...  4.54 us
    pallas_call x1, Pallas kernels, local(): pl.pallas_call(factor, in_specs=[smem, smem, smem, vmem], out_specs=[vmem...  3.77 us
    pallas_call x1, Pallas kernels, local(): pl.pallas_call(span_inverse, in_specs=[smem, smem, smem] + [vmem] * 10, o...  2.83 us
    pallas_call x1, Pallas kernels, local(): pl.pallas_call(span_forward, in_specs=[smem, smem, smem] + [vmem] * 5, ou...  2.38 us
  transfers between devices with their start and end apart: 1, of which 1 were waited for; matrix products, arithmetic and copies ran while one was open for 0% of the time, Pallas kernels for 6%

profile of v3, /device:TPU:32, one launch (start us, length us, event | category | flops | bytes accessed | tf_op | source)
XLA Modules:
  0.0 67.9 jit_solution(16242342708929889293)
XLA Ops:
  0.0 0.0 copy-start.9
  0.0 0.0 copy-start.4
  0.0 0.0 copy-start
  0.0 0.0 copy-start.8
  0.0 0.0 copy-start.7
  0.1 0.1 pad_add_fusion.place_ref
  0.2 0.1 add_add_fusion.1.sigma_ref
  0.3 6.5 %local_forward.1 = (f32[48,16,512]{2,1,0:T(8,128)}, f32[48,16,256]{2,1,0:T(8,128)}, f32[32,16,128]{2,1,0:T(8,128)}) custom-call(s32[2]{0:T(128)S(1)} %pad_add_fusion.place_ref, f32[384]{0:T(512)} %lower_ref.9, f32[384]{0:T(512)} %upper_ref.9, f32[16,256]{1,0:T(8,128)S(1)} %add_add_fusion.1.sigma_ref, f32[2,16,512]{2,1,0:T(8,128)} %constant.102.clone.weight_ref, ...), custom_call_target="tpu_custom_call" | custom-call | tf_op jit(solution)/shard_map/local_forward/pallas_call | solution.py:490
  6.8 11.2 %all-to-all-start = ((f32[32,16,128]{2,1,0:T(8,128)}), f32[32,16,128]{2,1,0:T(8,128)S(1)}, u32[]{:S(2)}, u32[]{:S(2)}) async-start(f32[32,16,128]{2,1,0:T(8,128)} %get-tuple-element.16), calls=%async_computation | async-start | bytes 524288 | tf_op jit(solution)/shard_map/all_to_all | solution.py:472
  18.0 0.1 subtract_multiply_fusion
  18.0 0.0 copy-done.9
  18.0 0.1 add_add_fusion.waves_ref
  18.1 0.0 copy-done.8
  18.1 0.0 copy-done.7
  18.1 3.8 %factor.1 = (f32[2,48,8,512]{3,2,1,0:T(8,128)S(1)}, f32[8,8,512]{2,1,0:T(8,128)S(1)}, f32[8,8,512]{2,1,0:T(8,128)S(1)}, f32[4,8,512]{2,1,0:T(8,128)S(1)}) custom-call(s32[2]{0:T(128)S(1)} %pad_add_fusion.place_ref, f32[384]{0:T(512)S(1)} %copy-done.7, f32[384]{0:T(512)S(1)} %copy-done.8, f32[8,512]{1,0:T(8,128)S(1)} %add_add_fusion.waves_ref), custom_call_target="tpu_custom_call" | custom-call | tf_op jit(solution)/shard_map/factor/pallas_call | solution.py:516
  21.9 8.2 %all-to-all-done.piece_ref = f32[32,16,128]{2,1,0:T(8,128)S(1)} async-done(((f32[32,16,128]{2,1,0:T(8,128)}), f32[32,16,128]{2,1,0:T(8,128)S(1)}, u32[]{:S(2)}, u32[]{:S(2)}) %all-to-all-start) | async-done | bytes 262176 | tf_op jit(solution)/shard_map/all_to_all | solution.py:472
  30.1 0.0 copy-done.4
  30.1 0.0 copy-done
  30.1 2.4 %span_forward.1 = (f32[48,16,512]{2,1,0:T(8,128)S(1)}, f32[8,16,512]{2,1,0:T(8,128)S(1)}, f32[48,16,128]{2,1,0:T(8,128)S(1)}, f32[2,16,512]{2,1,0:T(8,128)S(1)}) custom-call(s32[2]{0:T(128)S(1)} %pad_add_fusion.place_ref, f32[384]{0:T(512)S(1)} %copy-done.7, f32[384]{0:T(512)S(1)} %copy-done.8, f32[32,16,128]{2,1,0:T(8,128)S(1)} %all-to-all-done.piece_ref, ...), custom_call_target="tpu_custom_call" | custom-call | tf_op jit(solution)/shard_map/span_forward/pallas_call | solution.py:531
  32.5 11.8 %all_to_all.15.ends_ref = f32[8,16,512]{2,1,0:T(8,128)S(1)} all-to-all(f32[8,16,512]{2,1,0:T(8,128)S(1)} %get-tuple-element.20), channel_id=1, replica_groups=mesh['row'=32,'col'=8] {'col'}, dimensions={0} | all-to-all | bytes 524288 | tf_op jit(solution)/shard_map/all_to_all | solution.py:472
  44.3 0.0 copy-start.1
  44.3 0.0 copy-start.2
  44.3 0.0 copy-start.3
  44.3 0.0 copy-start.5
  44.3 0.0 copy-start.6
  44.3 2.8 %span_inverse.1 = f32[32,16,128]{2,1,0:T(8,128)S(1)} custom-call(s32[2]{0:T(128)S(1)} %pad_add_fusion.place_ref, f32[384]{0:T(512)S(1)} %copy-done.7, f32[384]{0:T(512)S(1)} %copy-done.8, f32[48,16,512]{2,1,0:T(8,128)S(1)} %get-tuple-element.19.rows_ref, f32[8,16,512]{2,1,0:T(8,128)S(1)} %all_to_all.15.ends_ref, ...), custom_call_target="tpu_custom_call" | custom-call | tf_op jit(solution)/shard_map/span_inverse/pallas_call | solution.py:546
  47.2 16.1 %all_to_all.16.piece_ref = f32[32,16,128]{2,1,0:T(8,128)S(1)} all-to-all(f32[32,16,128]{2,1,0:T(8,128)S(1)} %span_inverse.1), channel_id=1, replica_groups=mesh['row'=32,'col'=8] {'row'}, dimensions={0} | all-to-all | bytes 524288 | tf_op jit(solution)/shard_map/all_to_all | solution.py:472
  63.3 0.0 copy-done.1
  63.3 0.0 copy-done.2
  63.3 0.0 copy-done.3
  63.3 0.0 copy-done.5
  63.3 0.0 copy-done.6
  63.3 4.5 %local_inverse.1 = f32[48,16,512]{2,1,0:T(8,128)} custom-call(s32[2]{0:T(128)S(1)} %pad_add_fusion.place_ref, f32[384]{0:T(512)S(1)} %copy-done.7, f32[384]{0:T(512)S(1)} %copy-done.8, f32[32,16,128]{2,1,0:T(8,128)S(1)} %all_to_all.16.piece_ref, f32[48,16,512]{2,1,0:T(8,128)S(1)} %copy-done.2, f32[48,16,256]{2,1,0:T(8,128)S(1)} %copy-done.5, ...), custom_call_target="tpu_custom_call" | custom-call | tf_op jit(solution)/shard_map/local_inverse/pallas_call | solution.py:557
  (2 shorter events, 0.1 us)
Async XLA Ops:
  0.0 18.0 %copy-start.9 = (f32[512]{0:T(512)S(1)}, f32[512]{0:T(512)}, u32[]{:S(2)}) copy-start(f32[512]{0:T(512)} %constant.112) | copy-start | bytes 6148
  0.0 30.1 %copy-start.4 = (bf16[2,128,512]{2,1,0:T(8,128)(2,1)S(1)}, bf16[2,128,512]{2,1,0:T(8,128)(2,1)}, u32[]{:S(2)}) copy-start(bf16[2,128,512]{2,1,0:T(8,128)(2,1)} %constant.113.plane_ref) | copy-start | bytes 786436
  0.0 30.1 %copy-start = (bf16[2,512,512]{2,1,0:T(8,128)(2,1)S(1)}, bf16[2,512,512]{2,1,0:T(8,128)(2,1)}, u32[]{:S(2)}) copy-start(bf16[2,512,512]{2,1,0:T(8,128)(2,1)} %constant.101.clone.cell_ref) | copy-start | bytes 3145732
  0.0 18.1 %copy-start.8 = (f32[384]{0:T(512)S(1)}, f32[384]{0:T(512)}, u32[]{:S(2)}) copy-start(f32[384]{0:T(512)} %upper_ref.9) | copy-start | bytes 4612
  0.0 18.1 %copy-start.7 = (f32[384]{0:T(512)S(1)}, f32[384]{0:T(512)}, u32[]{:S(2)}) copy-start(f32[384]{0:T(512)} %lower_ref.9) | copy-start | bytes 4612
  6.8 23.4 %all-to-all-start = ((f32[32,16,128]{2,1,0:T(8,128)}), f32[32,16,128]{2,1,0:T(8,128)S(1)}, u32[]{:S(2)}, u32[]{:S(2)}) async-start(f32[32,16,128]{2,1,0:T(8,128)} %get-tuple-element.16), calls=%async_computation | async-start | bytes 524288 | tf_op jit(solution)/shard_map/all_to_all | solution.py:472
  44.3 19.0 %copy-start.1 = (bf16[2,2,256,256]{3,2,1,0:T(8,128)(2,1)S(1)}, bf16[2,2,256,256]{3,2,1,0:T(8,128)(2,1)}, u32[]{:S(2)}) copy-start(bf16[2,2,256,256]{3,2,1,0:T(8,128)(2,1)} %constant.98.clone.stream_ref) | copy-start | bytes 1572868
  44.3 19.0 %copy-start.2 = (f32[48,16,512]{2,1,0:T(8,128)S(1)}, f32[48,16,512]{2,1,0:T(8,128)}, u32[]{:S(2)}) copy-start(f32[48,16,512]{2,1,0:T(8,128)} %get-tuple-element.25.rows_ref) | copy-start | bytes 4718596
  44.3 19.0 %copy-start.3 = (bf16[2,256,256]{2,1,0:T(8,128)(2,1)S(1)}, bf16[2,256,256]{2,1,0:T(8,128)(2,1)}, u32[]{:S(2)}) copy-start(bf16[2,256,256]{2,1,0:T(8,128)(2,1)} %constant.99.clone.sine_ref) | copy-start | bytes 786436
  44.3 19.0 %copy-start.5 = (f32[48,16,256]{2,1,0:T(8,128)S(1)}, f32[48,16,256]{2,1,0:T(8,128)}, u32[]{:S(2)}) copy-start(f32[48,16,256]{2,1,0:T(8,128)} %get-tuple-element.26.inv_ref) | copy-start | bytes 2359300
  44.3 19.0 %copy-start.6 = (f32[2,16,512]{2,1,0:T(8,128)S(1)}, f32[2,16,512]{2,1,0:T(8,128)}, u32[]{:S(2)}) copy-start(f32[2,16,512]{2,1,0:T(8,128)} %constant.102.clone.weight_ref) | copy-start | bytes 196612
